TPU v7x, 256 devices: a whole 4x4x8 slice. The times are simulated.
256 devices in a mesh: dp: 32 (over z, y), seq: 8 (over x, core).
Axes of the slice: x: 4, y: 4, z: 8, core: 2. Of those that a mesh axis runs over, the one named last changes fastest.
Arguments:
- prefill_queries: bfloat16 [32768, 4096], P(('dp', 'seq')), may hold values from -8 to 8
- prefill_key_values: bfloat16 [32768, 2048], P(('dp', 'seq')), may hold values from -8 to 8
- decode_queries: bfloat16 [32, 4096], P('dp', 'seq'), may hold values from -8 to 8
- decode_key_values: bfloat16 [32, 2048], P('dp', 'seq'), may hold values from -8 to 8
- arrival: int32 [32], replicated, may hold values from 0 to 31, as said below
- pooled_key_values: bfloat16 [1024, 128, 2048], P('dp', None, 'seq'), may hold values from -8 to 8
- page_table: int32 [32, 32], P('dp'), may hold values from 0 to 31, as said below
- cache_len: int32 [32], P('dp'), may hold values from 1 to 4096, as said below
- mover: int32 [32], P('dp'), may hold values from 0 to 0, as said below
Outputs:
- prefill_out: bfloat16 [32768, 4096], P(('dp', 'seq'))
- decode_out: bfloat16 [32, 4096], P('dp', 'seq')
- received_pages: bfloat16 [1024, 128, 2048], P('dp', None, 'seq')
Inputs may be any that keep to these rules, and one draw needn't show every extreme that they name: `arrival`: every decode request appears exactly once. `page_table`: the 1 request of one group together name each of that group's 32 pages exactly once. `cache_len`: some request has exactly 4096 cached tokens in every draw. `mover`: the request with the most cached tokens always moves.
All inputs are finite; a program needn't handle non-finite values.
Results may differ from a plain program's by a relative error of at most 0.006.
Values may be sent and summed in bfloat16 or wider, within the bound.
A program may use at most 64 MiB of HBM per device.

v0:
```python
import math

import jax
import jax.numpy as jnp
from jax import lax
from jax.sharding import PartitionSpec as P

QUERY_HEADS = 32
KV_HEAD_COUNT = 8
HEAD_SIZE = 128


NEG_FILL = -1e30


def passed_along(block, axis, distance):
    devices = range(lax.axis_size(axis))
    route = [((i - distance) % len(devices), i) for i in devices]
    return lax.ppermute(block, axis, route)


def keys_attention(prefill_queries, prefill_key_values):
    group_local_rows = prefill_queries.shape[0]
    group_extent = QUERY_HEADS // KV_HEAD_COUNT
    query_rows = prefill_queries.reshape(group_local_rows, KV_HEAD_COUNT, group_extent, HEAD_SIZE)
    row_offset = lax.axis_index("seq") * group_local_rows
    scale_factor = 1.0 / math.sqrt(HEAD_SIZE)
    query_pos = row_offset + lax.broadcasted_iota(jnp.int32, (group_local_rows, 1), 0)
    state_dimensions = (KV_HEAD_COUNT, group_extent, group_local_rows)
    portion_slice = lax.all_gather(prefill_key_values, "seq", axis=0, tiled=True)
    first_index = jnp.int32(0)
    run_max = jnp.full(state_dimensions, NEG_FILL, jnp.float32)
    run_total = jnp.zeros(state_dimensions, jnp.float32)
    run_acc = jnp.zeros(state_dimensions + (HEAD_SIZE,), jnp.float32)
    portion_rows = portion_slice.shape[0]
    key_value_rows = portion_slice.reshape(portion_rows, KV_HEAD_COUNT, 2 * HEAD_SIZE)
    for first_key in range(0, portion_rows, 512):
        width_now = min(512, portion_rows - first_key)
        key_block = key_value_rows[first_key : first_key + width_now]
        scores = (
            jnp.einsum(
                "qngd,knd->ngqk",
                query_rows,
                key_block[:, :, :HEAD_SIZE],
                preferred_element_type=jnp.float32,
            )
            * scale_factor
        )
        key_pos = first_index + first_key + lax.broadcasted_iota(jnp.int32, (1, width_now), 1)
        allowed = key_pos <= query_pos
        masked = jnp.where(allowed, scores, NEG_FILL)
        new_max = jnp.maximum(run_max, jnp.max(masked, axis=-1))
        rescale = jnp.exp(run_max - new_max)
        weights = jnp.where(allowed, jnp.exp(masked - new_max[..., None]), 0.0).astype(jnp.bfloat16)
        run_total = run_total * rescale + jnp.sum(weights, axis=-1, dtype=jnp.float32)
        run_acc = run_acc * rescale[..., None] + jnp.einsum(
            "ngqk,knd->ngqd",
            weights,
            key_block[:, :, HEAD_SIZE:],
            preferred_element_type=jnp.float32,
        )
        run_max = new_max
    normed = run_acc / run_total[..., None]
    return (
        jnp.transpose(normed, (2, 0, 1, 3))
        .astype(jnp.bfloat16)
        .reshape(group_local_rows, QUERY_HEADS * HEAD_SIZE)
    )


def decode_attention(
    decode_queries, decode_key_values, arrival, pooled_key_values, page_table, cache_len
):
    request_count = decode_queries.shape[0]
    kv_local = decode_key_values.shape[1] // (2 * HEAD_SIZE)
    group_extent = QUERY_HEADS // KV_HEAD_COUNT
    query_all, pair_all = (
        lax.all_gather(decode_queries, "dp", axis=0, tiled=True),
        lax.all_gather(decode_key_values, "dp", axis=0, tiled=True),
    )
    total_rows = query_all.shape[0]
    wanted = lax.axis_index("dp") * request_count + lax.broadcasted_iota(
        jnp.int32, (request_count, 1), 0
    )
    row_ids = lax.broadcasted_iota(jnp.int32, (request_count, total_rows), 1)
    decode_row = jnp.sum(jnp.where(arrival[None, :] == wanted, row_ids, 0), axis=1)
    query_sel = jnp.take(query_all, decode_row, axis=0).reshape(
        request_count, kv_local, group_extent, HEAD_SIZE
    )
    pair_sel = jnp.take(pair_all, decode_row, axis=0).reshape(
        request_count, kv_local, 2 * HEAD_SIZE
    )
    cache_row_list = jnp.take(pooled_key_values, page_table, axis=0)
    cache_row_list = cache_row_list.reshape(request_count, -1, kv_local, 2 * HEAD_SIZE)
    span_rows = cache_row_list.shape[1]
    scale_factor = 1.0 / math.sqrt(HEAD_SIZE)
    cached_scores = (
        jnp.einsum(
            "rngd,rtnd->rngt",
            query_sel,
            cache_row_list[..., :HEAD_SIZE],
            preferred_element_type=jnp.float32,
        )
        * scale_factor
    )
    new_scores = (
        jnp.einsum(
            "rngd,rnd->rng",
            query_sel,
            pair_sel[..., :HEAD_SIZE],
            preferred_element_type=jnp.float32,
        )
        * scale_factor
    )
    valid_rows = (
        lax.broadcasted_iota(jnp.int32, (request_count, 1, 1, span_rows), 3)
        < cache_len[:, None, None, None]
    )
    masked = jnp.where(valid_rows, cached_scores, NEG_FILL)
    row_max = jnp.maximum(jnp.max(masked, axis=-1), new_scores)
    cached_weights = jnp.where(valid_rows, jnp.exp(masked - row_max[..., None]), 0.0).astype(
        jnp.bfloat16
    )
    new_weights = jnp.exp(new_scores - row_max).astype(jnp.bfloat16)
    wide_new = new_weights.astype(jnp.float32)
    totals = jnp.sum(cached_weights, axis=-1, dtype=jnp.float32) + wide_new
    summed = jnp.einsum(
        "rngt,rtnd->rngd",
        cached_weights,
        cache_row_list[..., HEAD_SIZE:],
        preferred_element_type=jnp.float32,
    )
    summed = (
        summed + wide_new[..., None] * pair_sel[..., HEAD_SIZE:].astype(jnp.float32)[:, :, None, :]
    )
    return (
        (summed / totals[..., None])
        .astype(jnp.bfloat16)
        .reshape(request_count, kv_local * group_extent * HEAD_SIZE)
    )


def move_pages(pooled_key_values, page_table, cache_len, mover):
    mover_slot = mover[0]
    moving_table = lax.dynamic_index_in_dim(page_table, mover_slot, 0, keepdims=False)
    moving_len = lax.dynamic_index_in_dim(cache_len, mover_slot, 0, keepdims=False)
    page_rows = jnp.take(pooled_key_values, moving_table, axis=0)
    live_pages = (
        lax.broadcasted_iota(jnp.int32, (page_rows.shape[0], 1, 1), 0) * page_rows.shape[1]
        < moving_len
    )
    page_rows = jnp.where(live_pages, page_rows, jnp.zeros_like(page_rows))
    return passed_along(page_rows, "dp", 1)


def on_device(
    prefill_queries,
    prefill_key_values,
    decode_queries,
    decode_key_values,
    arrival,
    pooled_key_values,
    page_table,
    cache_len,
    mover,
):
    prefill_out = keys_attention(prefill_queries, prefill_key_values)
    decode_out = decode_attention(
        decode_queries, decode_key_values, arrival, pooled_key_values, page_table, cache_len
    )
    received_pages = move_pages(pooled_key_values, page_table, cache_len, mover)
    return (prefill_out, decode_out, received_pages)


def solution(mesh):
    placed = (
        P(("dp", "seq"), None),
        P(("dp", "seq"), None),
        P("dp", "seq"),
        P("dp", "seq"),
        P(),
        P("dp", None, "seq"),
        P("dp", None),
        P("dp"),
        P("dp"),
    )
    return jax.shard_map(
        on_device,
        mesh=mesh,
        in_specs=placed,
        out_specs=(P(("dp", "seq"), None), P("dp", "seq"), P("dp", None, "seq")),
        check_vma=False,
    )
```

profile of v0, /device:TPU:4, one launch (start us, length us, event | category | flops | bytes accessed | tf_op | source)
XLA Modules:
  0.0 181.2 jit_solution(11569675293962441517)
XLA Ops:
  7.2 2.2 %copy.26 = bf16[128,2048]{0,1:T(8,128)(2,1)} copy(bf16[128,2048]{1,0:T(8,128)(2,1)} %param.10) | data formatting | bytes 1048576 | tf_op args[1]
  10.1 0.7 fusion.23
  10.8 2.0 %gather_fusion.1 = bf16[32,128,256]{2,1,0:T(8,128)(2,1)} fusion(bf16[32,128,256]{2,1,0:T(8,128)(2,1)S(1)} %copy-done, s32[1024]{0:T(1024)S(1)} %pad_clamp_fusion), kind=kCustom, calls=%fused_computation.1 | custom fusion | bytes 4194432 | tf_op jit(solution)/shard_map/jit(_take)/gather | solution.py:147
  12.8 3.3 %select_select_fusion = bf16[32,128,256]{2,1,0:T(8,128)(2,1)} fusion(bf16[32,128,256]{2,1,0:T(8,128)(2,1)} %gather_fusion.1, pred[32]{0:T(512)(128)(4,1)S(1)} %get-tuple-element.57, pred[32]{0:T(512)(128)(4,1)S(1)} %get-tuple-element.58), kind=kLoop, calls=%fused_computation.17 | loop fusion | flops 2097152 | bytes 4194368 | tf_op jit(solution)/shard_map/jit(_where)/select_n | solution.py:152
  16.0 1.6 collective-permute-start
  17.6 1.8 reshape.261
  19.5 2.0 %gather_fusion = bf16[32,128,256]{2,1,0:T(8,128)(2,1)} fusion(bf16[32,128,256]{2,1,0:T(8,128)(2,1)S(1)} %copy-done, s32[1024]{0:T(1024)S(1)} %pad_clamp_fusion.1), kind=kCustom, calls=%fused_computation | custom fusion | bytes 4194432 | tf_op jit(solution)/shard_map/jit(_take)/gather | solution.py:93
  21.6 1.9 %broadcast_select_fusion = bf16[1,4096,1,256]{3,1,2,0:T(8,128)(2,1)S(1)} fusion(bf16[1,4096,1,256]{3,1,2,0:T(8,128)(2,1)} %bitcast.141, pred[4096]{0:T(1024)(128)(4,1)S(1)} %broadcast_bitcast_fusion), kind=kLoop, calls=%fused_computation.18 | loop fusion | flops 1048576 | bytes 4198400 | tf_op jit(solution)/shard_map/jit(_take)/select_n | solution.py:93
  23.5 0.6 fusion.22
  26.1 84.3 %all-gather = bf16[32,1,512]{2,1,0:T(2,128)(2,1)S(1)} all-gather(bf16[1,1,512]{2,1,0:T(2,128)(2,1)S(1)} %bitcast.147), channel_id=1, replica_groups=mesh['dp'=32,'seq'=8] {'dp'}, dimensions={0}, use_global_device_ids=true | all-gather | bytes 33792 | tf_op jit(solution)/shard_map/all_gather | solution.py:78
  110.4 41.7 %all-gather.1 = bf16[32,1,256]{2,1,0:T(2,128)(2,1)S(1)} all-gather(bf16[1,1,256]{2,1,0:T(2,128)(2,1)S(1)} %bitcast.149), channel_id=1, replica_groups=mesh['dp'=32,'seq'=8] {'dp'}, dimensions={0}, use_global_device_ids=true | all-gather | bytes 16896 | tf_op jit(solution)/shard_map/all_gather | solution.py:79
  152.2 0.5 fusion.30
  152.8 0.2 convert_reduce_fusion.2
  153.0 0.3 fusion.8
  153.3 0.6 copy.52
  153.9 0.1 broadcast_compare_fusion
  154.1 2.5 %fusion.29 = (bf16[512,2048]{0,1:T(8,128)(2,1)S(1)}, bf16[512,2048]{0,1:T(8,128)(2,1)S(1)}) fusion(bf16[1024,2048]{0,1:T(8,128)(2,1)} %all-gather.4.cloned.1.call-done), kind=kLoop, calls=%fused_computation.77 | loop fusion | bytes 8388608 | tf_op jit(solution)/shard_map/slice | solution.py:39
  156.6 2.1 %fusion = (f32[8,4,128]{2,1,0:T(4,128)S(1)}, f32[8,512,128,4]{2,1,3,0:T(8,128)S(1)}) fusion(pred[128,512]{0,1:T(8,128)(4,1)S(1)} %get-tuple-element.46, bf16[128,8,4,128]{3,2,1,0:T(4,128)(2,1)S(1)} %reshape.261, bf16[512,8,256]{0,2,1:T(8,128)(2,1)S(1)} %bitcast.144), kind=kOutput, calls=%fused_computation.8 | convolution fusion | flops 543158272 | bytes 10567680 | tf_op jit(solution)/shard_map/qngd,knd->ngqk/dot_general | solution.py:41
  158.6 2.1 %fusion.1 = (f32[8,4,128]{2,1,0:T(4,128)S(1)}, f32[8,512,128,4]{2,1,3,0:T(8,128)S(1)}) fusion(pred[128,512]{0,1:T(8,128)(4,1)S(1)} %get-tuple-element.45, bf16[128,8,4,128]{3,2,1,0:T(4,128)(2,1)S(1)} %reshape.261, bf16[512,8,256]{0,2,1:T(8,128)(2,1)S(1)} %bitcast.142), kind=kOutput, calls=%fused_computation.9 | convolution fusion | flops 543158272 | bytes 10567680 | tf_op jit(solution)/shard_map/qngd,knd->ngqk/dot_general | solution.py:41
  160.7 2.2 %fusion.11 = f32[8,4,128,128]{2,3,1,0:T(8,128)S(1)} fusion(bf16[512,8,256]{0,2,1:T(8,128)(2,1)S(1)} %bitcast.145, f32[8,512,128,4]{2,1,3,0:T(8,128)S(1)} %get-tuple-element.50, f32[8,4,128]{2,1,0:T(4,128)S(1)} %get-tuple-element.44, pred[128,512]{0,1:T(8,128)(4,1)S(1)} %get-tuple-element.46), kind=kOutput, calls=%fused_computation.31 | convolution fusion | flops 547356672 | bytes 11616256 | tf_op jit(solution)/shard_map/ngqk,knd->ngqd/dot_general | solution.py:56
  162.9 4.5 %convert_reduce_fusion = (f32[8,4,128]{2,1,0:T(4,128)S(1)}, f32[8,4,128]{2,1,0:T(4,128)S(1)}) fusion(f32[8,4,128]{2,1,0:T(4,128)S(1)} %get-tuple-element.43, f32[8,512,128,4]{2,1,3,0:T(8,128)S(1)} %get-tuple-element.48, pred[128,512]{0,1:T(8,128)(4,1)S(1)} %get-tuple-element.45, f32[8,4,128]{2,1,0:T(4,128)S(1)} %get-tuple-element.44, ...), kind=kLoop, calls=%fused_computation.4 | loop fusion | flops 29351936 | bytes 16973824 | tf_op jit(solution)/shard_map/reduce_sum | solution.py:55
  167.4 2.5 %fusion.4 = bf16[128,8,4,128]{0,3,2,1:T(8,128)(2,1)S(1)} fusion(f32[8,4,128,128]{2,3,1,0:T(8,128)S(1)} %fusion.11, bf16[512,8,256]{0,2,1:T(8,128)(2,1)S(1)} %bitcast.143, f32[128,8,4]{0,2,1:T(4,128)S(1)} %get-tuple-element.38, f32[128,8,4]{0,2,1:T(4,128)S(1)} %get-tuple-element.39, f32[128,8,4]{0,2,1:T(4,128)S(1)} %get-tuple-element.42, ...), kind=kOutput, calls=%fused_computation.14 | convolution fusion | flops 549978112 | bytes 12713984 | tf_op jit(solution)/shard_map/ngqk,knd->ngqd/dot_general | solution.py:56
  169.9 1.3 copy.33
  171.2 3.1 %copy.55 = bf16[32,128,256]{2,1,0:T(8,128)(2,1)} copy(bf16[32,128,256]{2,1,0:T(8,128)(2,1)} %collective-permute-done) | data formatting | bytes 4194304
  (30 shorter events, 0.4 us)
Async XLA Ops:
  7.2 3.6 %copy-start = (bf16[32,128,256]{2,1,0:T(8,128)(2,1)S(1)}, bf16[32,128,256]{2,1,0:T(8,128)(2,1)}, u32[]{:S(2)}) copy-start(bf16[32,128,256]{2,1,0:T(8,128)(2,1)} %param.14) | copy-start | bytes 6291460
  7.2 5.6 %copy-start.3 = (s32[1,32]{1,0:T(1,128)S(1)}, s32[1,32]{1,0:T(1,128)}, u32[]{:S(2)}) copy-start(s32[1,32]{1,0:T(1,128)} %param.15) | copy-start | bytes 388
  7.2 146.9 %all-gather.4.cloned.1.call-start = ((), (), s32[]{:S(2)}) async-start(), calls=%async_computation | async-start | bytes 4718592 | tf_op jit(solution)/shard_map/all_gather | solution.py:30
  16.0 138.0 %collective-permute-start = (bf16[32,128,256]{2,1,0:T(8,128)(2,1)}, bf16[32,128,256]{2,1,0:T(8,128)(2,1)}, u32[]{:S(2)}, u32[]{:S(2)}) collective-permute-start(bf16[32,128,256]{2,1,0:T(8,128)(2,1)} %select_select_fusion), channel_id=1, source_target_pairs={{248,0},{0,8},{8,16},{16,24},{24,32},{32,40},{40,48},{48,56},{56,6... | collective-permute-start | bytes 6291464 | tf_op jit(solution)/shard_map/ppermute | solution.py:19
  19.4 4.1 %copy-start.4 = (s32[32]{0:T(128)S(1)}, s32[32]{0:T(128)}, u32[]{:S(2)}) copy-start(s32[32]{0:T(128)} %param.13) | copy-start | bytes 388
  19.5 6.7 %copy-start.1 = (bf16[1,512]{1,0:T(2,128)(2,1)S(1)}, bf16[1,512]{1,0:T(2,128)(2,1)}, u32[]{:S(2)}) copy-start(bf16[1,512]{1,0:T(2,128)(2,1)} %param.11) | copy-start | bytes 3076
  19.5 90.9 %copy-start.2 = (bf16[1,256]{1,0:T(2,128)(2,1)S(1)}, bf16[1,256]{1,0:T(2,128)(2,1)}, u32[]{:S(2)}) copy-start(bf16[1,256]{1,0:T(2,128)(2,1)} %param.12) | copy-start | bytes 1540
Sparse Core Ops, SparseCore 0:
  10.4 40.4 all-gather.3
where the time goes:
time: 182 us; the launch traced here: 181 us
  blocking collectives  126 us (69%)
  between operations  16.8 us (9%)
  local copies, waits for them, and re-layouts  15.6 us (9%)
  other arithmetic  11.5 us (6%)
  matrix products  9.68 us (5%)
    all_gather x1, blocking collectives, decode_attention(): lax.all_gather(decode_queries, 'dp', axis=0, tiled=True)  84.3 us
    all_gather x1, blocking collectives, decode_attention(): lax.all_gather(decode_key_values, 'dp', axis=0, tiled=True)  41.7 us
    unnamed x14, local copies, waits for them, and re-layouts  7.25 us
    dot_general x2, matrix products, keys_attention(): jnp.einsum('ngqk,knd->ngqd', weights, key_block[:, :, HEAD_SIZE:], prefer...  4.67 us
    reduce_sum x1, other arithmetic, keys_attention(): jnp.sum(weights, axis=-1, dtype=jnp.float32)  4.47 us
    dot_general x2, matrix products, keys_attention(): jnp.einsum('qngd,knd->ngqk', query_rows, key_block[:, :, :HEAD_SIZE], pre...  4.15 us
  transfers between devices with their start and end apart: 2, of which 0 were waited for; matrix products, arithmetic and copies ran while one was open for 8% of the time, Pallas kernels for 0%

commit v1 on v0

v1 whole, which is shorter than its diff:
```python
import functools
import math

import jax
import jax.numpy as jnp
from jax import lax
from jax.experimental import pallas as pl
from jax.experimental.pallas import tpu as pltpu
from jax.sharding import PartitionSpec as P

QUERY_HEADS = 32
KV_HEAD_COUNT = 8
HEAD_SIZE = 128
GROUP_EXTENT = QUERY_HEADS // KV_HEAD_COUNT
NEG_FILL = -1e30
SCALE = 1.0 / math.sqrt(HEAD_SIZE)
MESH = pl.DeviceIdType.MESH
Y_CHIPS = 4
Z_CHIPS = 8
HALF = 64


def exchange_kernel(
    kv_ref,
    query_ref,
    pair_ref,
    table_ref,
    len_ref,
    all_kv_ref,
    all_query_ref,
    all_pair_ref,
    near_table_ref,
    near_len_ref,
    kv_recv,
    kv_send,
    part_recv,
    part_send,
    own_sem,
    row_recv,
    row_send,
    block_recv,
    block_send,
    meta_recv,
    meta_send,
):
    group = lax.axis_index("dp")
    member = lax.axis_index("seq")
    z, y = group // Y_CHIPS, group % Y_CHIPS
    x, core = member // 2, member % 2
    next_group = (group + 1) % (Y_CHIPS * Z_CHIPS)

    def at(g, m):
        return (g, m)

    peers = [at(group, 2 * x + 1 - core)]
    for hop in (1, 3):
        peers.append(at(group, 2 * ((x + hop) % 4) + core))
    for hop in range(1, Y_CHIPS):
        peers.append(at(z * Y_CHIPS + (y + hop) % Y_CHIPS, member))
    for hop in range(1, Z_CHIPS):
        peers.append(at(((z + hop) % Z_CHIPS) * Y_CHIPS + y, member))
    previous_group = (group + Y_CHIPS * Z_CHIPS - 1) % (Y_CHIPS * Z_CHIPS)
    peers.append(at(next_group, member))
    peers.append(at(previous_group, member))
    barrier = pltpu.get_barrier_semaphore()
    for peer in peers:
        pl.semaphore_signal(barrier, inc=1, device_id=peer, device_id_type=MESH)
    pl.semaphore_wait(barrier, len(peers))

    def kv_copy(source, chip, half, target, lane):
        rows = pl.ds(half * HALF, HALF)
        return pltpu.make_async_remote_copy(
            src_ref=source.at[rows],
            dst_ref=all_kv_ref.at[2 * chip + core, rows],
            send_sem=kv_send.at[lane],
            recv_sem=kv_recv.at[chip, half],
            device_id=target,
            device_id_type=MESH,
        )

    def part_copy(source, chip, half):
        rows = pl.ds(half * HALF, HALF)
        return pltpu.make_async_remote_copy(
            src_ref=source.at[rows],
            dst_ref=all_kv_ref.at[2 * chip + core, rows],
            send_sem=part_send.at[chip, half],
            recv_sem=part_recv.at[chip, half],
            device_id=at(group, 2 * x + 1 - core),
            device_id_type=MESH,
        )

    def chip_at(c):
        return at(group, 2 * c + core)

    def held(chip):
        return all_kv_ref.at[2 * chip + core]

    @pl.when(x < 3)
    def _():
        for half in range(2):
            kv_copy(kv_ref, x, half, chip_at(x + 1), half).start()

    @pl.when(x == 0)
    def _():
        for half in range(2):
            kv_copy(kv_ref, x, half, chip_at(3), 2 + half).start()

    @pl.when(x == 1)
    def _():
        kv_copy(kv_ref, x, 1, chip_at(0), 2).start()

    for half in range(2):
        part_copy(kv_ref, x, half).start()
    own = pltpu.make_async_copy(kv_ref, all_kv_ref.at[member], own_sem)
    own.start()

    metas = []
    for index, (source, target) in enumerate(
        ((table_ref, near_table_ref), (len_ref, near_len_ref))
    ):
        metas.append(
            pltpu.make_async_remote_copy(
                src_ref=source,
                dst_ref=target,
                send_sem=meta_send.at[index],
                recv_sem=meta_recv.at[index],
                device_id=at(next_group, member),
                device_id_type=MESH,
            )
        )
        metas[-1].start()

    rows_out = []
    for index, (source, target) in enumerate(
        ((query_ref, all_query_ref), (pair_ref, all_pair_ref))
    ):
        mine = pltpu.make_async_copy(source, target.at[z, y], row_recv.at[index, 0])
        mine.start()
        rows_out.append(mine)
        for hop in range(1, Y_CHIPS):
            copy = pltpu.make_async_remote_copy(
                src_ref=source,
                dst_ref=target.at[z, y],
                send_sem=row_send.at[index, hop],
                recv_sem=row_recv.at[index, hop],
                device_id=at(z * Y_CHIPS + (y + hop) % Y_CHIPS, member),
                device_id_type=MESH,
            )
            copy.start()
            rows_out.append(copy)
    for copy in rows_out:
        copy.wait()
    blocks_out = []
    for index, target in enumerate((all_query_ref, all_pair_ref)):
        for hop in range(1, Z_CHIPS):
            copy = pltpu.make_async_remote_copy(
                src_ref=target.at[z],
                dst_ref=target.at[z],
                send_sem=block_send.at[index, hop],
                recv_sem=block_recv.at[index, hop],
                device_id=at(((z + hop) % Z_CHIPS) * Y_CHIPS + y, member),
                device_id_type=MESH,
            )
            copy.start()
            blocks_out.append(copy)

    def arrived(chip, half):
        kv_copy(kv_ref, chip, half, chip_at(0), 0).wait_recv()

    @pl.when(x == 0)
    def _():
        arrived(1, 1)
        kv_copy(held(1), 1, 1, chip_at(3), 4).start()
        for lane in range(5):
            kv_copy(kv_ref, x, 0, chip_at(1), lane).wait_send()

    @pl.when(x == 1)
    def _():
        for half in range(2):
            arrived(0, half)
            part_copy(held(0), 0, half).start()
        for lane in range(3):
            kv_copy(kv_ref, x, 0, chip_at(0), lane).wait_send()

    @pl.when(x == 2)
    def _():
        arrived(1, 0)
        kv_copy(held(1), 1, 0, chip_at(3), 2).start()
        part_copy(held(1), 1, 0).start()
        arrived(1, 1)
        part_copy(held(1), 1, 1).start()
        for half in range(2):
            arrived(0, half)
            part_copy(held(0), 0, half).start()
        for lane in range(3):
            kv_copy(kv_ref, x, 0, chip_at(3), lane).wait_send()

    @pl.when(x == 3)
    def _():
        for half in range(2):
            arrived(0, half)
            kv_copy(held(0), 0, half, chip_at(2), half).start()
            part_copy(held(0), 0, half).start()
            arrived(2, half)
            part_copy(held(2), 2, half).start()
        for half in range(2):
            arrived(1, half)
            part_copy(held(1), 1, half).start()
        for lane in range(2):
            kv_copy(kv_ref, x, 0, chip_at(2), lane).wait_send()

    for chip in range(4):

        @pl.when(chip <= x)
        def _():
            for half in range(2):
                part_copy(kv_ref, chip, half).wait()

    for copy in blocks_out + metas:
        copy.wait()
    own.wait()


def exchange(kv, query, pair, table, lens):
    any_space = pl.BlockSpec(memory_space=pl.ANY)
    dma = pltpu.SemaphoreType.DMA
    return pl.pallas_call(
        exchange_kernel,
        out_shape=(
            jax.ShapeDtypeStruct((8,) + kv.shape, kv.dtype),
            jax.ShapeDtypeStruct((Z_CHIPS, Y_CHIPS) + query.shape, query.dtype),
            jax.ShapeDtypeStruct((Z_CHIPS, Y_CHIPS) + pair.shape, pair.dtype),
            jax.ShapeDtypeStruct(table.shape, table.dtype),
            jax.ShapeDtypeStruct(lens.shape, lens.dtype),
        ),
        in_specs=[any_space] * 5,
        out_specs=(any_space,) * 5,
        scratch_shapes=[
            dma((4, 2)),
            dma((5,)),
            dma((4, 2)),
            dma((4, 2)),
            dma,
            dma((2, 4)),
            dma((2, 4)),
            dma((2, 8)),
            dma((2, 8)),
            dma((2,)),
            dma((2,)),
        ],
        compiler_params=pltpu.CompilerParams(collective_id=0, has_side_effects=True),
        name="exchange",
    )(kv, query, pair, table, lens)


def prefill_kernel(query_ref, kv_ref, out_ref):
    member = lax.axis_index("seq")
    x, core = member // 2, member % 2
    rows = query_ref.shape[0]

    def attend(chips):
        keys = 256 * chips
        key = kv_ref[:keys, :HEAD_SIZE]
        value = jnp.concatenate(
            [kv_ref[:keys, HEAD_SIZE:], jnp.ones((keys, HEAD_SIZE), jnp.bfloat16)], axis=1
        )
        allowed = lax.broadcasted_iota(jnp.int32, (rows, 256), 1) <= (
            core * 128 + lax.broadcasted_iota(jnp.int32, (rows, 256), 0)
        )
        for g in range(GROUP_EXTENT):
            columns = slice(g * HEAD_SIZE, (g + 1) * HEAD_SIZE)
            scores = lax.dot_general(
                query_ref[:, columns],
                key,
                (((1,), (1,)), ((), ())),
                preferred_element_type=jnp.float32,
            )
            last = jnp.where(allowed, scores[:, keys - 256 :], NEG_FILL)
            if chips > 1:
                scores = jnp.concatenate([scores[:, : keys - 256], last], axis=1)
            else:
                scores = last
            top = jnp.max(scores, axis=1, keepdims=True)
            weights = jnp.exp((scores - top) * SCALE).astype(jnp.bfloat16)
            summed = jnp.dot(weights, value, preferred_element_type=jnp.float32)
            out_ref[:, columns] = (summed[:, :HEAD_SIZE] / summed[:, HEAD_SIZE:]).astype(
                jnp.bfloat16
            )

    for chips in range(1, 5):
        pl.when(x == chips - 1)(functools.partial(attend, chips))


def prefill(query, all_kv):
    rows = query.shape[0]
    return pl.pallas_call(
        prefill_kernel,
        grid=(KV_HEAD_COUNT,),
        out_shape=jax.ShapeDtypeStruct(query.shape, query.dtype),
        in_specs=[
            pl.BlockSpec((rows, GROUP_EXTENT * HEAD_SIZE), lambda n: (0, n)),
            pl.BlockSpec((all_kv.shape[0], 2 * HEAD_SIZE), lambda n: (0, n)),
        ],
        out_specs=pl.BlockSpec((rows, GROUP_EXTENT * HEAD_SIZE), lambda n: (0, n)),
        cost_estimate=pl.CostEstimate(
            flops=4 * rows * 1024 * QUERY_HEADS * HEAD_SIZE,
            bytes_accessed=6 << 20,
            transcendentals=rows * 1024 * QUERY_HEADS,
        ),
        name="prefill",
    )(query, all_kv)


def decode_kernel(
    arrival_ref, table_ref, len_ref, query_ref, pair_ref, pool_ref, out_ref, cache_ref, sems
):
    pages, tokens = pool_ref.shape[0], pool_ref.shape[1]
    cached = pages * tokens
    copies = []
    for i in range(pages):
        copies.append(
            pltpu.make_async_copy(
                pool_ref.at[table_ref[0, i]],
                cache_ref.at[pl.ds(i * tokens, tokens)],
                sems.at[i],
            )
        )
        copies[-1].start()
    me = lax.axis_index("dp")
    row = jnp.int32(0)
    for i in range(arrival_ref.shape[0]):
        row = jnp.where(arrival_ref[i] == me, i, row)
    flat = query_ref[row].astype(jnp.float32)
    query = jnp.concatenate(
        [flat[:, g * HEAD_SIZE : (g + 1) * HEAD_SIZE] for g in range(GROUP_EXTENT)]
        + [jnp.zeros((8 - GROUP_EXTENT, HEAD_SIZE), jnp.float32)],
        axis=0,
    ).astype(jnp.bfloat16)
    pair = jnp.broadcast_to(pair_ref[row].astype(jnp.float32), (tokens, 2 * HEAD_SIZE))
    first = lax.broadcasted_iota(jnp.int32, pair.shape, 0) == 0
    cache_ref[cached:, :] = jnp.where(first, pair, 0.0).astype(jnp.bfloat16)
    for copy in copies:
        copy.wait()
    scores = lax.dot_general(
        query,
        cache_ref[:, :HEAD_SIZE],
        (((1,), (1,)), ((), ())),
        preferred_element_type=jnp.float32,
    )
    spot = lax.broadcasted_iota(jnp.int32, scores.shape, 1)
    scores = jnp.where((spot < len_ref[0]) | (spot == cached), scores, NEG_FILL)
    top = jnp.max(scores, axis=1, keepdims=True)
    weights = jnp.exp((scores - top) * SCALE).astype(jnp.bfloat16)
    value = jnp.concatenate(
        [cache_ref[:, HEAD_SIZE:], jnp.ones((cached + tokens, HEAD_SIZE), jnp.bfloat16)], axis=1
    )
    summed = jnp.dot(weights, value, preferred_element_type=jnp.float32)
    normed = summed[:, :HEAD_SIZE] / summed[:, HEAD_SIZE:]
    for g in range(GROUP_EXTENT):
        out_ref[:, g * HEAD_SIZE : (g + 1) * HEAD_SIZE] = normed[g : g + 1].astype(jnp.bfloat16)


def decode(arrival, table, lens, query, pair, pool):
    pages, tokens, width = pool.shape
    smem = pl.BlockSpec(memory_space=pltpu.SMEM)
    vmem = pl.BlockSpec(memory_space=pltpu.VMEM)
    return pl.pallas_call(
        decode_kernel,
        out_shape=jax.ShapeDtypeStruct((1, query.shape[-1]), jnp.bfloat16),
        in_specs=[smem, smem, smem, vmem, vmem, pl.BlockSpec(memory_space=pl.ANY)],
        out_specs=vmem,
        scratch_shapes=[
            pltpu.VMEM(((pages + 1) * tokens, width), jnp.bfloat16),
            pltpu.SemaphoreType.DMA((pages,)),
        ],
        cost_estimate=pl.CostEstimate(
            flops=1 << 27, bytes_accessed=2 << 20, transcendentals=1 << 15
        ),
        name="decode",
    )(arrival, table, lens, query, pair, pool)


def place_kernel(table_ref, len_ref, raw_ref, out_ref, held_ref, zero_ref, in_sems, out_sems):
    pages, tokens = raw_ref.shape[0], raw_ref.shape[1]
    for i in range(pages):
        pltpu.make_async_copy(
            raw_ref.at[table_ref[0, i]], held_ref.at[i], in_sems.at[i]
        ).start()
    zero_ref[...] = jnp.zeros_like(zero_ref)
    for i in range(pages):
        pltpu.make_async_copy(raw_ref.at[0], held_ref.at[i], in_sems.at[i]).wait()
        live = i * tokens < len_ref[0]

        @pl.when(live)
        def _():
            pltpu.make_async_copy(held_ref.at[i], out_ref.at[i], out_sems.at[i]).start()

        @pl.when(jnp.logical_not(live))
        def _():
            pltpu.make_async_copy(zero_ref, out_ref.at[i], out_sems.at[i]).start()

    for i in range(pages):
        pltpu.make_async_copy(zero_ref, out_ref.at[i], out_sems.at[i]).wait()


def place_pages(table, lens, raw):
    pages = raw.shape[0]
    smem = pl.BlockSpec(memory_space=pltpu.SMEM)
    any_space = pl.BlockSpec(memory_space=pl.ANY)
    return pl.pallas_call(
        place_kernel,
        out_shape=jax.ShapeDtypeStruct(raw.shape, raw.dtype),
        in_specs=[smem, smem, any_space],
        out_specs=any_space,
        scratch_shapes=[
            pltpu.VMEM(raw.shape, raw.dtype),
            pltpu.VMEM(raw.shape[1:], raw.dtype),
            pltpu.SemaphoreType.DMA((pages,)),
            pltpu.SemaphoreType.DMA((pages,)),
        ],
        cost_estimate=pl.CostEstimate(flops=0, bytes_accessed=4 << 20, transcendentals=0),
        name="place_pages",
    )(table, lens, raw)


def on_device(
    prefill_queries,
    prefill_key_values,
    decode_queries,
    decode_key_values,
    arrival,
    pooled_key_values,
    page_table,
    cache_len,
    mover,
):
    groups = lax.axis_size("dp")
    raw = lax.ppermute(
        pooled_key_values, "dp", [((i - 1) % groups, i) for i in range(groups)]
    )
    moving_table = lax.dynamic_slice_in_dim(page_table, mover[0], 1, 0)
    moving_len = lax.dynamic_slice_in_dim(cache_len, mover[0], 1, 0)
    all_kv, all_query, all_pair, near_table, near_len = exchange(
        prefill_key_values, decode_queries, decode_key_values, moving_table, moving_len
    )
    prefill_out = prefill(prefill_queries, all_kv.reshape(-1, all_kv.shape[-1]))
    decode_out = decode(
        arrival,
        page_table,
        cache_len,
        all_query.reshape((groups,) + decode_queries.shape),
        all_pair.reshape((groups,) + decode_key_values.shape),
        pooled_key_values,
    )
    received_pages = place_pages(near_table, near_len, raw)
    return (prefill_out, decode_out, received_pages)


def solution(mesh):
    placed = (
        P(("dp", "seq"), None),
        P(("dp", "seq"), None),
        P("dp", "seq"),
        P("dp", "seq"),
        P(),
        P("dp", None, "seq"),
        P("dp", None),
        P("dp"),
        P("dp"),
    )
    return jax.shard_map(
        on_device,
        mesh=mesh,
        in_specs=placed,
        out_specs=(P(("dp", "seq"), None), P("dp", "seq"), P("dp", None, "seq")),
        check_vma=False,
    )
```

time: 182 us -> 87 us (0.48)
  blocking collectives: 126 us -> 0 us
  Pallas kernels: 0 us -> 81.6 us
  between operations: 16.8 us -> 1.3 us
  local copies, waits for them, and re-layouts: 15.6 us -> 1.34 us
  other arithmetic: 11.5 us -> 0 us
  matrix products: 9.68 us -> 0 us
    all_gather x2 -> x0, blocking collectives: 126 us -> none  [the longest x1 84.3 us: decode_attention(): lax.all_gather(decode_queries, 'dp', axis=0, tiled=True)]
    pallas_call x0 -> x4, Pallas kernels: none -> 81.6 us  [the longest x1 62.9 us: exchange(): pl.pallas_call(exchange_kernel, out_shape=(jax.ShapeDtypeStruct((8,) + kv...]
    dot_general x7 -> x0, matrix products: 9.68 us -> none  [the longest x2 4.67 us: keys_attention(): jnp.einsum('ngqk,knd->ngqd', weights, key_block[:, :, HEAD_SIZE:], prefer...]
    unnamed x14 -> x2, local copies, waits for them, and re-layouts: 7.25 us -> 1.34 us
    select_n x5 -> x0, other arithmetic: 5.91 us -> none  [the longest x1 3.28 us: move_pages(): page_rows = jnp.where(live_pages, page_rows, jnp.zeros_like(page_rows))]
    reduce_sum x3 -> x0, other arithmetic: 5.33 us -> none  [the longest x1 4.47 us: keys_attention(): jnp.sum(weights, axis=-1, dtype=jnp.float32)]
    gather x2 -> x0, local copies, waits for them, and re-layouts: 4 us -> none  [the longest x1 2 us: move_pages(): page_rows = jnp.take(pooled_key_values, moving_table, axis=0)]
    slice x1 -> x0, local copies, waits for them, and re-layouts: 2.5 us -> none  [keys_attention(): key_block = key_value_rows[first_key:first_key + width_now]]
  transfers between devices with their start and end apart: 2 -> 1, of which waited for: 0 -> 0; matrix products, arithmetic and copies ran while one was open for 8% -> 0% of each run, Pallas kernels for 0% -> 90%
where the time goes in v1:
time: 87 us; the launch traced here: 85.9 us
  Pallas kernels  81.6 us (94%)
  starting transfers between devices  1.65 us (2%)
  local copies, waits for them, and re-layouts  1.34 us (2%)
  between operations  1.3 us (1%)
    pallas_call x1, Pallas kernels, exchange(): pl.pallas_call(exchange_kernel, out_shape=(jax.ShapeDtypeStruct((8,) + kv...  62.9 us
    pallas_call x1, Pallas kernels, prefill(): pl.pallas_call(prefill_kernel, grid=(KV_HEAD_COUNT,), out_shape=jax.Shape...  10 us
    pallas_call x1, Pallas kernels, decode(): pl.pallas_call(decode_kernel, out_shape=jax.ShapeDtypeStruct((1, query.sh...  4.7 us
    pallas_call x1, Pallas kernels, place_pages(): pl.pallas_call(place_kernel, out_shape=jax.ShapeDtypeStruct(raw.shape, ra...  4 us
  transfers between devices with their start and end apart: 1, of which 0 were waited for; matrix products, arithmetic and copies ran while one was open for 0% of the time, Pallas kernels for 90%

profile of v1, /device:TPU:4, one launch (start us, length us, event | category | flops | bytes accessed | tf_op | source)
XLA Modules:
  0.0 85.9 jit_solution(11543623372740492877)
XLA Ops:
  0.6 1.7 %collective-permute-start = (bf16[32,128,256]{2,1,0:T(8,128)(2,1)}, bf16[32,128,256]{2,1,0:T(8,128)(2,1)S(1)}, u32[]{:S(2)}, u32[]{:S(2)}) collective-permute-start(bf16[32,128,256]{2,1,0:T(8,128)(2,1)} %pool_ref.1), channel_id=1, source_target_pairs={{248,0},{0,8},{8,16},{16,24},{24,32},{32,40},{40,48},{48,56},{56,6... | collective-permute-start | bytes 6291464 | tf_op jit(solution)/shard_map/ppermute | solution.py:438
  2.9 62.9 %exchange.1 = (bf16[8,128,2048]{2,1,0:T(8,128)(2,1)}, bf16[8,4,1,512]{3,2,1,0:T(2,128)(2,1)}, bf16[8,4,1,256]{3,2,1,0:T(2,128)(2,1)}, s32[1,32]{1,0:T(1,128)}, s32[1]{0:T(128)}) custom-call(bf16[128,2048]{1,0:T(8,128)(2,1)} %kv_ref.1, bf16[1,512]{1,0:T(2,128)(2,1)} %query_ref.2, bf16[1,256]{1,0:T(2,128)(2,1)} %pair_ref.1, s32[1,32]{1,0:T(1,128)} %table_ref.2, ...), custom_call_target="tpu_custom_call" | custom-call | tf_op jit(solution)/shard_map/exchange/pallas_call | solution.py:227
  65.8 4.7 %decode.1 = bf16[1,512]{1,0:T(2,128)(2,1)} custom-call(s32[32]{0:T(128)} %arrival_ref.1, s32[1,32]{1,0:T(1,128)} %table_ref.2, s32[1]{0:T(128)S(6)} %copy.11.len_ref, bf16[32,1,512]{2,1,0:T(2,128)(2,1)} %bitcast.3, bf16[32,1,256]{2,1,0:T(2,128)(2,1)} %bitcast.4, bf16[32,128,256]{2,1,0:T(8,128)(2,1)} %pool_ref.1), custom_call_target="tpu_custom_call" | custom-call | flops 134217728 | bytes 2097152 | tf_op jit(solution)/shard_map/decode/pallas_call | solution.py:367
  70.5 10.0 %prefill.1 = bf16[128,4096]{1,0:T(8,128)(2,1)} custom-call(bf16[128,4096]{1,0:T(8,128)(2,1)} %query_ref.3, bf16[1024,2048]{1,0:T(8,128)(2,1)} %bitcast.5), custom_call_target="tpu_custom_call" | custom-call | flops 2147483648 | bytes 6291456 | tf_op jit(solution)/shard_map/prefill/pallas_call | solution.py:296
  80.6 0.0 collective-permute-done.raw_ref
  80.6 0.0 copy-start
  80.6 1.3 %copy-done = bf16[32,128,256]{2,1,0:T(8,128)(2,1)} copy-done((bf16[32,128,256]{2,1,0:T(8,128)(2,1)}, bf16[32,128,256]{2,1,0:T(8,128)(2,1)S(1)}, u32[]{:S(2)}) %copy-start) | copy-done | bytes 2097176
  81.9 4.0 %place_pages.1 = bf16[32,128,256]{2,1,0:T(8,128)(2,1)} custom-call(s32[1,32]{1,0:T(1,128)} %get-tuple-element.11.table_ref, s32[1]{0:T(128)} %get-tuple-element.12.len_ref, bf16[32,128,256]{2,1,0:T(8,128)(2,1)} %copy-done), custom_call_target="tpu_custom_call" | custom-call | bytes 4194304 | tf_op jit(solution)/shard_map/place_pages/pallas_call | solution.py:410
Async XLA Ops:
  0.6 79.9 %collective-permute-start = (bf16[32,128,256]{2,1,0:T(8,128)(2,1)}, bf16[32,128,256]{2,1,0:T(8,128)(2,1)S(1)}, u32[]{:S(2)}, u32[]{:S(2)}) collective-permute-start(bf16[32,128,256]{2,1,0:T(8,128)(2,1)} %pool_ref.1), channel_id=1, source_target_pairs={{248,0},{0,8},{8,16},{16,24},{24,32},{32,40},{40,48},{48,56},{56,6... | collective-permute-start | bytes 6291464 | tf_op jit(solution)/shard_map/ppermute | solution.py:438
  80.6 1.3 %copy-start = (bf16[32,128,256]{2,1,0:T(8,128)(2,1)}, bf16[32,128,256]{2,1,0:T(8,128)(2,1)S(1)}, u32[]{:S(2)}) copy-start(bf16[32,128,256]{2,1,0:T(8,128)(2,1)S(1)} %collective-permute-done.raw_ref) | copy-start | bytes 6291460

commit v2 on v0

v2 whole, which is shorter than its diff:
```python
import functools
import math

import jax
import jax.numpy as jnp
from jax import lax
from jax.experimental import pallas as pl
from jax.experimental.pallas import tpu as pltpu
from jax.sharding import PartitionSpec as P

QUERY_HEADS = 32
KV_HEAD_COUNT = 8
HEAD_SIZE = 128
GROUP_EXTENT = QUERY_HEADS // KV_HEAD_COUNT
NEG_FILL = -1e30
SCALE = 1.0 / math.sqrt(HEAD_SIZE)
MESH = pl.DeviceIdType.MESH
Y_CHIPS = 4
Z_CHIPS = 8
HALF = 64
FORWARD_PAGES = 24
PIECES = 2


def exact_dot(left, right, dimensions):
    return lax.dot_general(
        left, right, (dimensions, ((), ())), preferred_element_type=jnp.float32
    )


def main_kernel(
    arrival_ref,
    table_ref,
    len_ref,
    query_ref,
    kv_ref,
    row_query_ref,
    row_pair_ref,
    pool_ref,
    move_table_ref,
    move_len_ref,
    prefill_ref,
    decode_ref,
    raw_ref,
    near_table_ref,
    near_len_ref,
    queries,
    kv_all,
    pool,
    outs,
    all_query,
    all_pair,
    decode_out,
    relays,
    load_sems,
    out_sems,
    kv_recv,
    kv_send,
    part_recv,
    part_send,
    row_recv,
    row_send,
    meta_recv,
    meta_send,
    page_recv,
    page_send,
    relay_recv,
    relay_send,
):
    group = lax.axis_index("dp")
    member = lax.axis_index("seq")
    z, y = group // Y_CHIPS, group % Y_CHIPS
    x, core = member // 2, member % 2
    groups = Y_CHIPS * Z_CHIPS
    rows = kv_ref.shape[0]
    pages, tokens, width = pool_ref.shape

    def chip_at(c):
        return (group, 2 * c + core)

    def same_member(g):
        return (g % groups, member)

    partner = (group, 2 * x + 1 - core)
    next_group = same_member(group + 1)
    first_hop = same_member(z * Y_CHIPS + (y + 3) % Y_CHIPS)
    step_up = jnp.where(y == 2, 1, 0)
    second_hop = same_member((z + step_up) * Y_CHIPS + (y + 3) % Y_CHIPS)

    def slot(c, half):
        return kv_all.at[pl.ds((2 * c + core) * rows + half * HALF, HALF)]

    def load(index, source, target):
        return pltpu.make_async_copy(source, target, load_sems.at[index])

    loads = [
        load(0, kv_ref, kv_all.at[pl.ds(member * rows, rows)]),
        load(1, row_query_ref, all_query.at[group]),
        load(2, row_pair_ref, all_pair.at[group]),
        load(3, pool_ref, pool),
        load(4, query_ref, queries),
    ]
    for copy in loads:
        copy.start()

    barrier = pltpu.get_barrier_semaphore()
    peers = [same_member(group + hop) for hop in range(1, groups)]
    peers += [partner, chip_at((x + 1) % 4), chip_at((x + 3) % 4)]
    for peer in peers:
        pl.semaphore_signal(barrier, inc=1, device_id=peer, device_id_type=MESH)
    pl.semaphore_wait(barrier, len(peers))

    def remote(source, target, send_sem, recv_sem, device):
        return pltpu.make_async_remote_copy(
            src_ref=source,
            dst_ref=target,
            send_sem=send_sem,
            recv_sem=recv_sem,
            device_id=device,
            device_id_type=MESH,
        )

    def row_copy(index, hop):
        source, target = ((row_query_ref, all_query), (row_pair_ref, all_pair))[index]
        return remote(
            source,
            target.at[group],
            row_send.at[index, hop],
            row_recv.at[index, hop],
            same_member(group + hop),
        )

    for hop in range(1, groups):
        for index in range(2):
            row_copy(index, hop).start()
    metas = [
        remote(move_table_ref, near_table_ref, meta_send.at[0], meta_recv.at[0], next_group),
        remote(move_len_ref, near_len_ref, meta_send.at[1], meta_recv.at[1], next_group),
    ]
    for copy in metas:
        copy.start()

    def kv_copy(c, half, target, lane):
        return remote(
            slot(c, half), slot(c, half), kv_send.at[lane], kv_recv.at[c, half], target
        )

    def part_copy(c, half):
        return remote(
            slot(c, half), slot(c, half), part_send.at[c, half], part_recv.at[c, half], partner
        )

    loads[0].wait()

    @pl.when(x < 3)
    def _():
        for half in range(2):
            kv_copy(x, half, chip_at(x + 1), half).start()

    @pl.when(x == 0)
    def _():
        for half in range(2):
            kv_copy(x, half, chip_at(3), 2 + half).start()

    @pl.when(x == 1)
    def _():
        kv_copy(x, 1, chip_at(0), 2).start()

    for half in range(2):
        part_copy(x, half).start()

    straight = []
    for index in range(PIECES):
        count = FORWARD_PAGES // PIECES
        part = pl.ds(index * count, count)
        straight.append(
            remote(
                pool_ref.at[part],
                raw_ref.at[part],
                page_send.at[index],
                page_recv.at[index],
                next_group,
            )
        )
        straight[-1].start()
    per_piece = (pages - FORWARD_PAGES) // PIECES

    def relay_copy(step, index):
        here = pl.ds(index * per_piece, per_piece)
        final = pl.ds(FORWARD_PAGES + index * per_piece, per_piece)
        source = pool_ref.at[final] if step == 0 else relays.at[step - 1, here]
        target = raw_ref.at[final] if step == 2 else relays.at[step, here]
        return remote(
            source,
            target,
            relay_send.at[step, index],
            relay_recv.at[step, index],
            second_hop if step == 1 else first_hop,
        )

    def relay(step, index):
        relay_copy(step - 1, index).wait_recv()
        relay_copy(step, index).start()

    for index in range(PIECES):
        relay_copy(0, index).start()

    def attend_decode():
        row = jnp.int32(0)
        for i in range(groups):
            row = jnp.where(arrival_ref[i] == group, i, row)
        flat = all_query[row].astype(jnp.float32)
        query = jnp.concatenate(
            [flat[:, g * HEAD_SIZE : (g + 1) * HEAD_SIZE] for g in range(GROUP_EXTENT)]
            + [jnp.zeros((8 - GROUP_EXTENT, HEAD_SIZE), jnp.float32)],
            axis=0,
        )
        pair = all_pair[row].astype(jnp.float32)
        cached = pool[...].reshape(pages * tokens, width)
        scores = exact_dot(
            query.astype(jnp.bfloat16), cached[:, :HEAD_SIZE], ((1,), (1,))
        )
        spot = lax.broadcasted_iota(jnp.int32, scores.shape, 1)
        page = lax.shift_right_logical(spot, 7)
        token = lax.bitwise_and(spot, tokens - 1)
        first_spot = jnp.zeros_like(spot)
        for i in range(pages):
            first_spot = jnp.where(page == table_ref[0, i], i * tokens, first_spot)
        scores = jnp.where(first_spot + token < len_ref[0], scores, NEG_FILL)
        new_score = jnp.sum(query * pair[:, :HEAD_SIZE], axis=1, keepdims=True)
        top = jnp.maximum(jnp.max(scores, axis=1, keepdims=True), new_score)
        weights = jnp.exp((scores - top) * SCALE).astype(jnp.bfloat16)
        new_weight = jnp.exp((new_score - top) * SCALE).astype(jnp.bfloat16).astype(jnp.float32)
        value = jnp.concatenate(
            [cached[:, HEAD_SIZE:], jnp.ones((pages * tokens, HEAD_SIZE), jnp.bfloat16)], axis=1
        )
        summed = exact_dot(weights, value, ((1,), (0,)))
        normed = (summed[:, :HEAD_SIZE] + new_weight * pair[:, HEAD_SIZE:]) / (
            summed[:, HEAD_SIZE:] + new_weight
        )
        for g in range(GROUP_EXTENT):
            decode_out[:, g * HEAD_SIZE : (g + 1) * HEAD_SIZE] = normed[g : g + 1].astype(
                jnp.bfloat16
            )

    for copy in loads[1:4]:
        copy.wait()
    for hop in range(1, groups):
        for index in range(2):
            row_copy(index, hop).wait()
    attend_decode()
    decode_store = pltpu.make_async_copy(decode_out, decode_ref, out_sems.at[KV_HEAD_COUNT])
    decode_store.start()

    def arrived(c, half):
        kv_copy(c, half, partner, 0).wait_recv()

    def take(c, half):
        arrived(c, half)
        part_copy(c, half).start()

    relay(1, 0)

    @pl.when(x == 1)
    def _():
        take(0, 0)

    @pl.when(x == 2)
    def _():
        arrived(1, 0)
        kv_copy(1, 0, chip_at(3), 2).start()
        part_copy(1, 0).start()

    @pl.when(x == 3)
    def _():
        arrived(0, 0)
        kv_copy(0, 0, chip_at(2), 0).start()
        part_copy(0, 0).start()
        take(2, 0)

    @pl.when(x == 0)
    def _():
        arrived(1, 1)
        kv_copy(1, 1, chip_at(3), 4).start()

    relay(1, 1)

    @pl.when(x == 1)
    def _():
        take(0, 1)

    @pl.when(x == 2)
    def _():
        take(1, 1)
        take(0, 0)

    @pl.when(x == 3)
    def _():
        arrived(0, 1)
        kv_copy(0, 1, chip_at(2), 1).start()
        part_copy(0, 1).start()
        take(2, 1)

    @pl.when(x == 2)
    def _():
        take(0, 1)

    @pl.when(x == 3)
    def _():
        take(1, 0)
        take(1, 1)

    relay(2, 0)
    for c in range(4):

        @pl.when(c <= x)
        def _():
            for half in range(2):
                part_copy(c, half).wait()

    loads[4].wait()

    def out_copy(n):
        columns = pl.ds(
            pl.multiple_of(n * GROUP_EXTENT * HEAD_SIZE, HEAD_SIZE), GROUP_EXTENT * HEAD_SIZE
        )
        return pltpu.make_async_copy(
            outs.at[:, columns], prefill_ref.at[:, columns], out_sems.at[n]
        )

    def attend(chips, n):
        keys = 256 * chips
        start = pl.multiple_of(n * 2 * HEAD_SIZE, HEAD_SIZE)
        key = kv_all[:keys, pl.ds(start, HEAD_SIZE)]
        value = jnp.concatenate(
            [
                kv_all[:keys, pl.ds(pl.multiple_of(start + HEAD_SIZE, HEAD_SIZE), HEAD_SIZE)],
                jnp.ones((keys, HEAD_SIZE), jnp.bfloat16),
            ],
            axis=1,
        )
        allowed = lax.broadcasted_iota(jnp.int32, (rows, 256), 1) <= (
            core * rows + lax.broadcasted_iota(jnp.int32, (rows, 256), 0)
        )
        for g in range(GROUP_EXTENT):
            columns = pl.ds(
                pl.multiple_of((n * GROUP_EXTENT + g) * HEAD_SIZE, HEAD_SIZE), HEAD_SIZE
            )
            scores = exact_dot(queries[:, columns], key, ((1,), (1,)))
            last = jnp.where(allowed, scores[:, keys - 256 :], NEG_FILL)
            if chips > 1:
                scores = jnp.concatenate([scores[:, : keys - 256], last], axis=1)
            else:
                scores = last
            top = jnp.max(scores, axis=1, keepdims=True)
            weights = jnp.exp((scores - top) * SCALE).astype(jnp.bfloat16)
            summed = exact_dot(weights, value, ((1,), (0,)))
            outs[:, columns] = (summed[:, :HEAD_SIZE] / summed[:, HEAD_SIZE:]).astype(
                jnp.bfloat16
            )

    def attend_head(n, carry):
        for chips in range(1, 5):
            pl.when(x == chips - 1)(functools.partial(attend, chips, n))
        out_copy(n).start()
        return carry

    middle = KV_HEAD_COUNT // 2
    lax.fori_loop(0, middle, attend_head, 0)
    relay(2, 1)
    lax.fori_loop(middle, KV_HEAD_COUNT, attend_head, 0)

    @pl.when(x == 0)
    def _():
        for lane in range(5):
            kv_copy(x, 0, chip_at(1), lane).wait_send()

    @pl.when((x == 1) | (x == 2))
    def _():
        for lane in range(3):
            kv_copy(x, 0, chip_at(3), lane).wait_send()

    @pl.when(x == 3)
    def _():
        for lane in range(2):
            kv_copy(x, 0, chip_at(2), lane).wait_send()

    decode_store.wait()

    def out_wait(n, carry):
        out_copy(n).wait()
        return carry

    lax.fori_loop(0, KV_HEAD_COUNT, out_wait, 0)
    for copy in metas:
        copy.wait()
    for index in range(PIECES):
        for step in range(3):
            relay_copy(step, index).wait_send()
        relay_copy(2, index).wait_recv()
    for copy in straight:
        copy.wait()


def attention_and_moves(
    arrival, table, lens, query, kv, row_query, row_pair, pool, move_table, move_len
):
    any_space = pl.BlockSpec(memory_space=pl.ANY)
    smem = pl.BlockSpec(memory_space=pltpu.SMEM)
    dma = pltpu.SemaphoreType.DMA
    groups = Y_CHIPS * Z_CHIPS
    pages = pool.shape[0]
    return pl.pallas_call(
        main_kernel,
        out_shape=(
            jax.ShapeDtypeStruct(query.shape, query.dtype),
            jax.ShapeDtypeStruct(row_query.shape, row_query.dtype),
            jax.ShapeDtypeStruct(pool.shape, pool.dtype),
            jax.ShapeDtypeStruct(move_table.shape, move_table.dtype),
            jax.ShapeDtypeStruct(move_len.shape, move_len.dtype),
        ),
        in_specs=[smem] * 3 + [any_space] * 7,
        out_specs=(any_space,) * 5,
        scratch_shapes=[
            pltpu.VMEM(query.shape, query.dtype),
            pltpu.VMEM((8 * kv.shape[0], kv.shape[1]), kv.dtype),
            pltpu.VMEM(pool.shape, pool.dtype),
            pltpu.VMEM(query.shape, query.dtype),
            pltpu.VMEM((groups,) + row_query.shape, row_query.dtype),
            pltpu.VMEM((groups,) + row_pair.shape, row_pair.dtype),
            pltpu.VMEM(row_query.shape, row_query.dtype),
            pltpu.VMEM((2, pages - FORWARD_PAGES) + pool.shape[1:], pool.dtype),
            dma((5,)),
            dma((KV_HEAD_COUNT + 1,)),
            dma((4, 2)),
            dma((5,)),
            dma((4, 2)),
            dma((4, 2)),
            dma((2, groups)),
            dma((2, groups)),
            dma((2,)),
            dma((2,)),
            dma((PIECES,)),
            dma((PIECES,)),
            dma((3, PIECES)),
            dma((3, PIECES)),
        ],
        compiler_params=pltpu.CompilerParams(collective_id=0, has_side_effects=True),
        name="attention_and_moves",
    )(arrival, table, lens, query, kv, row_query, row_pair, pool, move_table, move_len)


LOAD_PARTS = 4


def place_kernel(
    table_ref,
    len_ref,
    raw_ref,
    prefill_in,
    decode_in,
    out_ref,
    prefill_out,
    decode_out,
    table,
    lens,
    held,
    zero,
    passed,
    passed_row,
    in_sems,
    out_sems,
    meta_sems,
    pass_sems,
):
    pages, tokens = raw_ref.shape[0], raw_ref.shape[1]
    metas = [
        pltpu.make_async_copy(table_ref, table, meta_sems.at[0]),
        pltpu.make_async_copy(len_ref, lens, meta_sems.at[1]),
    ]
    for copy in metas:
        copy.start()
    count = pages // LOAD_PARTS
    parts = []
    for index in range(LOAD_PARTS):
        part = pl.ds(index * count, count)
        parts.append(
            pltpu.make_async_copy(raw_ref.at[part], held.at[part], in_sems.at[index])
        )
        parts[-1].start()
    into = [
        pltpu.make_async_copy(prefill_in, passed, pass_sems.at[0]),
        pltpu.make_async_copy(decode_in, passed_row, pass_sems.at[1]),
    ]
    back = [
        pltpu.make_async_copy(passed, prefill_out, pass_sems.at[2]),
        pltpu.make_async_copy(passed_row, decode_out, pass_sems.at[3]),
    ]
    for copy in into:
        copy.start()
    zero[...] = jnp.zeros_like(zero)
    for copy in metas + parts:
        copy.wait()
    for i in range(pages):
        live = i * tokens < lens[0]

        @pl.when(live)
        def _():
            pltpu.make_async_copy(held.at[table[0, i]], out_ref.at[i], out_sems.at[i]).start()

        @pl.when(jnp.logical_not(live))
        def _():
            pltpu.make_async_copy(zero, out_ref.at[i], out_sems.at[i]).start()

    for first, second in zip(into, back):
        first.wait()
        second.start()
    for i in range(pages):
        pltpu.make_async_copy(zero, out_ref.at[i], out_sems.at[i]).wait()
    for copy in back:
        copy.wait()


def place(table, lens, raw, prefill_rows, decode_rows):
    pages = raw.shape[0]
    any_space = pl.BlockSpec(memory_space=pl.ANY)
    dma = pltpu.SemaphoreType.DMA
    return pl.pallas_call(
        place_kernel,
        out_shape=tuple(
            jax.ShapeDtypeStruct(part.shape, part.dtype)
            for part in (raw, prefill_rows, decode_rows)
        ),
        in_specs=[any_space] * 5,
        out_specs=(any_space,) * 3,
        scratch_shapes=[
            pltpu.SMEM(table.shape, table.dtype),
            pltpu.SMEM(lens.shape, lens.dtype),
            pltpu.VMEM(raw.shape, raw.dtype),
            pltpu.VMEM(raw.shape[1:], raw.dtype),
            pltpu.VMEM(prefill_rows.shape, prefill_rows.dtype),
            pltpu.VMEM(decode_rows.shape, decode_rows.dtype),
            dma((LOAD_PARTS,)),
            dma((pages,)),
            dma((2,)),
            dma((4,)),
        ],
        name="place",
    )(table, lens, raw, prefill_rows, decode_rows)


def on_device(
    prefill_queries,
    prefill_key_values,
    decode_queries,
    decode_key_values,
    arrival,
    pooled_key_values,
    page_table,
    cache_len,
    mover,
):
    moving_table = lax.dynamic_slice_in_dim(page_table, mover[0], 1, 0)
    moving_len = lax.dynamic_slice_in_dim(cache_len, mover[0], 1, 0)
    prefill_rows, decode_rows, raw, near_table, near_len = attention_and_moves(
        arrival,
        page_table,
        cache_len,
        prefill_queries,
        prefill_key_values,
        decode_queries,
        decode_key_values,
        pooled_key_values,
        moving_table,
        moving_len,
    )
    received_pages, prefill_out, decode_out = place(
        near_table, near_len, raw, prefill_rows, decode_rows
    )
    return (prefill_out, decode_out, received_pages)


def solution(mesh):
    placed = (
        P(("dp", "seq"), None),
        P(("dp", "seq"), None),
        P("dp", "seq"),
        P("dp", "seq"),
        P(),
        P("dp", None, "seq"),
        P("dp", None),
        P("dp"),
        P("dp"),
    )
    return jax.shard_map(
        on_device,
        mesh=mesh,
        in_specs=placed,
        out_specs=(P(("dp", "seq"), None), P("dp", "seq"), P("dp", None, "seq")),
        check_vma=False,
    )
```

time: 182 us -> 63.6 us (0.35)
  blocking collectives: 126 us -> 0 us
  Pallas kernels: 0 us -> 62.2 us
  local copies, waits for them, and re-layouts: 15.6 us -> 0 us
  between operations: 16.8 us -> 1.29 us
  other arithmetic: 11.5 us -> 0 us
  matrix products: 9.68 us -> 0 us
    all_gather x2 -> x0, blocking collectives: 126 us -> none  [the longest x1 84.3 us: decode_attention(): lax.all_gather(decode_queries, 'dp', axis=0, tiled=True)]
    pallas_call x0 -> x2, Pallas kernels: none -> 62.2 us  [the longest x1 57.8 us: attention_and_moves(): pl.pallas_call(main_kernel, out_shape=(jax.ShapeDtypeStruct(query.shape,...]
    dot_general x7 -> x0, matrix products: 9.68 us -> none  [the longest x2 4.67 us: keys_attention(): jnp.einsum('ngqk,knd->ngqd', weights, key_block[:, :, HEAD_SIZE:], prefer...]
    unnamed x14 -> x0, local copies, waits for them, and re-layouts: 7.25 us -> none
    select_n x5 -> x0, other arithmetic: 5.91 us -> none  [the longest x1 3.28 us: move_pages(): page_rows = jnp.where(live_pages, page_rows, jnp.zeros_like(page_rows))]
    reduce_sum x3 -> x0, other arithmetic: 5.33 us -> none  [the longest x1 4.47 us: keys_attention(): jnp.sum(weights, axis=-1, dtype=jnp.float32)]
    gather x2 -> x0, local copies, waits for them, and re-layouts: 4 us -> none  [the longest x1 2 us: move_pages(): page_rows = jnp.take(pooled_key_values, moving_table, axis=0)]
    slice x1 -> x0, local copies, waits for them, and re-layouts: 2.5 us -> none  [keys_attention(): key_block = key_value_rows[first_key:first_key + width_now]]
  transfers between devices with their start and end apart: 2 -> 0, of which waited for: 0 -> 0; matrix products, arithmetic and copies ran while one was open for 8% -> 0% of each run, Pallas kernels for 0% -> 0%
where the time goes in v2:
time: 63.6 us; the launch traced here: 63.5 us
  Pallas kernels  62.2 us (98%)
  between operations  1.29 us (2%)
    pallas_call x1, Pallas kernels, attention_and_moves(): pl.pallas_call(main_kernel, out_shape=(jax.ShapeDtypeStruct(query.shape,...  57.8 us
    pallas_call x1, Pallas kernels, place(): pl.pallas_call(place_kernel, out_shape=tuple((jax.ShapeDtypeStruct(part.s...  4.4 us

profile of v2, /device:TPU:4, one launch (start us, length us, event | category | flops | bytes accessed | tf_op | source)
XLA Modules:
  0.0 63.5 jit_solution(7474553170082316189)
XLA Ops:
  1.3 57.8 %attention_and_moves.1 = (bf16[128,4096]{1,0:T(8,128)(2,1)}, bf16[1,512]{1,0:T(2,128)(2,1)}, bf16[32,128,256]{2,1,0:T(8,128)(2,1)}, s32[1,32]{1,0:T(1,128)}, s32[1]{0:T(128)}) custom-call(s32[32]{0:T(128)} %arrival_ref.1, s32[1,32]{1,0:T(1,128)} %move_table_ref, s32[1]{0:T(128)S(6)} %copy.11.len_ref.move_len_ref, bf16[128,4096]{1,0:T(8,128)(2,1)} %query_ref.1, ...), custom_call_target="tpu_custom_call" | custom-call | tf_op jit(solution)/shard_map/attention_and_moves/pallas_call | solution.py:413
  59.1 4.4 %place.1 = (bf16[32,128,256]{2,1,0:T(8,128)(2,1)}, bf16[128,4096]{1,0:T(8,128)(2,1)}, bf16[1,512]{1,0:T(2,128)(2,1)}) custom-call(s32[1,32]{1,0:T(1,128)} %get-tuple-element.11.table_ref, s32[1]{0:T(128)} %get-tuple-element.12.len_ref, bf16[32,128,256]{2,1,0:T(8,128)(2,1)} %get-tuple-element.13.raw_ref, bf16[128,4096]{1,0:T(8,128)(2,1)} %get-tuple-element.14.prefill_in, ...), custom_call_target="tpu_custom_call" | custom-call | tf_op jit(solution)/shard_map/place/pallas_call | solution.py:528

commit v3 on v2

--- a/solution.py
+++ b/solution.py
@@ -19,7 +19,8 @@
 Z_CHIPS = 8
 HALF = 64
 FORWARD_PAGES = 24
-PIECES = 2
+PIECES = 4
+FIRST_PAGES = 2
 
 
 def exact_dot(left, right, dimensions):
@@ -66,6 +67,8 @@
     page_send,
     relay_recv,
     relay_send,
+    up_recv,
+    up_send,
 ):
     group = lax.axis_index("dp")
     member = lax.axis_index("seq")
@@ -83,9 +86,8 @@
 
     partner = (group, 2 * x + 1 - core)
     next_group = same_member(group + 1)
-    first_hop = same_member(z * Y_CHIPS + (y + 3) % Y_CHIPS)
-    step_up = jnp.where(y == 2, 1, 0)
-    second_hop = same_member((z + step_up) * Y_CHIPS + (y + 3) % Y_CHIPS)
+    hop_down = same_member(z * Y_CHIPS + (y + 3) % Y_CHIPS)
+    hop_up = same_member(group + Y_CHIPS)
 
     def slot(c, half):
         return kv_all.at[pl.ds((2 * c + core) * rows + half * HALF, HALF)]
@@ -120,69 +122,16 @@
             device_id_type=MESH,
         )
 
-    def row_copy(index, hop):
-        source, target = ((row_query_ref, all_query), (row_pair_ref, all_pair))[index]
+    def straight_copy(index):
+        part = (pl.ds(0, FIRST_PAGES), pl.ds(FIRST_PAGES, FORWARD_PAGES - FIRST_PAGES))[index]
         return remote(
-            source,
-            target.at[group],
-            row_send.at[index, hop],
-            row_recv.at[index, hop],
-            same_member(group + hop),
-        )
-
-    for hop in range(1, groups):
-        for index in range(2):
-            row_copy(index, hop).start()
-    metas = [
-        remote(move_table_ref, near_table_ref, meta_send.at[0], meta_recv.at[0], next_group),
-        remote(move_len_ref, near_len_ref, meta_send.at[1], meta_recv.at[1], next_group),
-    ]
-    for copy in metas:
-        copy.start()
-
-    def kv_copy(c, half, target, lane):
-        return remote(
-            slot(c, half), slot(c, half), kv_send.at[lane], kv_recv.at[c, half], target
-        )
-
-    def part_copy(c, half):
-        return remote(
-            slot(c, half), slot(c, half), part_send.at[c, half], part_recv.at[c, half], partner
-        )
-
-    loads[0].wait()
-
-    @pl.when(x < 3)
-    def _():
-        for half in range(2):
-            kv_copy(x, half, chip_at(x + 1), half).start()
-
-    @pl.when(x == 0)
-    def _():
-        for half in range(2):
-            kv_copy(x, half, chip_at(3), 2 + half).start()
-
-    @pl.when(x == 1)
-    def _():
-        kv_copy(x, 1, chip_at(0), 2).start()
-
-    for half in range(2):
-        part_copy(x, half).start()
-
-    straight = []
-    for index in range(PIECES):
-        count = FORWARD_PAGES // PIECES
-        part = pl.ds(index * count, count)
-        straight.append(
-            remote(
-                pool_ref.at[part],
-                raw_ref.at[part],
-                page_send.at[index],
-                page_recv.at[index],
-                next_group,
-            )
-        )
-        straight[-1].start()
+            pool_ref.at[part],
+            raw_ref.at[part],
+            page_send.at[index],
+            page_recv.at[index],
+            next_group,
+        )
+
     per_piece = (pages - FORWARD_PAGES) // PIECES
 
     def relay_copy(step, index):
@@ -195,14 +144,100 @@
             target,
             relay_send.at[step, index],
             relay_recv.at[step, index],
-            second_hop if step == 1 else first_hop,
-        )
-
-    def relay(step, index):
-        relay_copy(step - 1, index).wait_recv()
-        relay_copy(step, index).start()
-
-    for index in range(PIECES):
+            hop_down,
+        )
+
+    def up_copy(index):
+        here = pl.ds(index * per_piece, per_piece)
+        return remote(
+            relays.at[0, here], relays.at[2, here], up_send.at[index], up_recv.at[index], hop_up
+        )
+
+    def raised_copy(index):
+        here = pl.ds(index * per_piece, per_piece)
+        return remote(
+            relays.at[2, here],
+            relays.at[1, here],
+            relay_send.at[1, index],
+            relay_recv.at[1, index],
+            hop_down,
+        )
+
+    def first_relay(index):
+        relay_copy(0, index).wait_recv()
+
+        @pl.when(y == 2)
+        def _():
+            up_copy(index).start()
+
+        @pl.when(y != 2)
+        def _():
+            relay_copy(1, index).start()
+
+    def raised_relay(index):
+        @pl.when(y == 2)
+        def _():
+            up_copy(index).wait_recv()
+            raised_copy(index).start()
+
+    def last_relay(index):
+        relay_copy(1, index).wait_recv()
+        relay_copy(2, index).start()
+
+    straight_copy(0).start()
+    relay_copy(0, 0).start()
+
+    def row_copy(index, hop):
+        source, target = ((row_query_ref, all_query), (row_pair_ref, all_pair))[index]
+        return remote(
+            source,
+            target.at[group],
+            row_send.at[index, hop],
+            row_recv.at[index, hop],
+            same_member(group + hop),
+        )
+
+    def kv_copy(c, half, target, lane):
+        return remote(
+            slot(c, half), slot(c, half), kv_send.at[lane], kv_recv.at[c, half], target
+        )
+
+    def part_copy(c, half):
+        return remote(
+            slot(c, half), slot(c, half), part_send.at[c, half], part_recv.at[c, half], partner
+        )
+
+    loads[0].wait()
+
+    @pl.when(x < 3)
+    def _():
+        for half in range(2):
+            kv_copy(x, half, chip_at(x + 1), half).start()
+
+    @pl.when(x == 0)
+    def _():
+        for half in range(2):
+            kv_copy(x, half, chip_at(3), 2 + half).start()
+
+    @pl.when(x == 1)
+    def _():
+        kv_copy(x, 1, chip_at(0), 2).start()
+
+    for half in range(2):
+        part_copy(x, half).start()
+
+    for hop in range(1, groups):
+        for index in range(2):
+            row_copy(index, hop).start()
+    metas = [
+        remote(move_table_ref, near_table_ref, meta_send.at[0], meta_recv.at[0], next_group),
+        remote(move_len_ref, near_len_ref, meta_send.at[1], meta_recv.at[1], next_group),
+    ]
+    for copy in metas:
+        copy.start()
+
+    straight_copy(1).start()
+    for index in range(1, PIECES):
         relay_copy(0, index).start()
 
     def attend_decode():
@@ -243,6 +278,58 @@
                 jnp.bfloat16
             )
 
+    def arrived(c, half):
+        kv_copy(c, half, partner, 0).wait_recv()
+
+    def take(c, half):
+        arrived(c, half)
+        part_copy(c, half).start()
+
+    first_relay(0)
+    first_relay(1)
+
+    @pl.when(x == 1)
+    def _():
+        take(0, 0)
+
+    @pl.when(x == 2)
+    def _():
+        arrived(1, 0)
+        kv_copy(1, 0, chip_at(3), 2).start()
+        part_copy(1, 0).start()
+
+    @pl.when(x == 3)
+    def _():
+        arrived(0, 0)
+        kv_copy(0, 0, chip_at(2), 0).start()
+        part_copy(0, 0).start()
+        take(2, 0)
+
+    @pl.when(x == 0)
+    def _():
+        arrived(1, 1)
+        kv_copy(1, 1, chip_at(3), 4).start()
+
+    raised_relay(0)
+    first_relay(2)
+    raised_relay(1)
+    first_relay(3)
+
+    @pl.when(x == 1)
+    def _():
+        take(0, 1)
+
+    @pl.when(x == 2)
+    def _():
+        take(1, 1)
+
+    @pl.when(x == 3)
+    def _():
+        arrived(0, 1)
+        kv_copy(0, 1, chip_at(2), 1).start()
+        part_copy(0, 1).start()
+        take(2, 1)
+
     for copy in loads[1:4]:
         copy.wait()
     for hop in range(1, groups):
@@ -252,57 +339,13 @@
     decode_store = pltpu.make_async_copy(decode_out, decode_ref, out_sems.at[KV_HEAD_COUNT])
     decode_store.start()
 
-    def arrived(c, half):
-        kv_copy(c, half, partner, 0).wait_recv()
-
-    def take(c, half):
-        arrived(c, half)
-        part_copy(c, half).start()
-
-    relay(1, 0)
-
-    @pl.when(x == 1)
+    raised_relay(2)
+    last_relay(0)
+    raised_relay(3)
+
+    @pl.when(x == 2)
     def _():
         take(0, 0)
-
-    @pl.when(x == 2)
-    def _():
-        arrived(1, 0)
-        kv_copy(1, 0, chip_at(3), 2).start()
-        part_copy(1, 0).start()
-
-    @pl.when(x == 3)
-    def _():
-        arrived(0, 0)
-        kv_copy(0, 0, chip_at(2), 0).start()
-        part_copy(0, 0).start()
-        take(2, 0)
-
-    @pl.when(x == 0)
-    def _():
-        arrived(1, 1)
-        kv_copy(1, 1, chip_at(3), 4).start()
-
-    relay(1, 1)
-
-    @pl.when(x == 1)
-    def _():
-        take(0, 1)
-
-    @pl.when(x == 2)
-    def _():
-        take(1, 1)
-        take(0, 0)
-
-    @pl.when(x == 3)
-    def _():
-        arrived(0, 1)
-        kv_copy(0, 1, chip_at(2), 1).start()
-        part_copy(0, 1).start()
-        take(2, 1)
-
-    @pl.when(x == 2)
-    def _():
         take(0, 1)
 
     @pl.when(x == 3)
@@ -310,7 +353,7 @@
         take(1, 0)
         take(1, 1)
 
-    relay(2, 0)
+    last_relay(1)
     for c in range(4):
 
         @pl.when(c <= x)
@@ -365,10 +408,13 @@
         out_copy(n).start()
         return carry
 
-    middle = KV_HEAD_COUNT // 2
-    lax.fori_loop(0, middle, attend_head, 0)
-    relay(2, 1)
-    lax.fori_loop(middle, KV_HEAD_COUNT, attend_head, 0)
+    def attend_then_relay(n, carry):
+        attend_head(n, carry)
+        pl.when(n == 1)(functools.partial(last_relay, 2))
+        pl.when(n == 3)(functools.partial(last_relay, 3))
+        return carry
+
+    lax.fori_loop(0, KV_HEAD_COUNT, attend_then_relay, 0)
 
     @pl.when(x == 0)
     def _():
@@ -397,9 +443,14 @@
     for index in range(PIECES):
         for step in range(3):
             relay_copy(step, index).wait_send()
+
+        @pl.when(y == 2)
+        def _():
+            up_copy(index).wait_send()
+
         relay_copy(2, index).wait_recv()
-    for copy in straight:
-        copy.wait()
+    for index in range(2):
+        straight_copy(index).wait()
 
 
 def attention_and_moves(
@@ -429,7 +480,7 @@
             pltpu.VMEM((groups,) + row_query.shape, row_query.dtype),
             pltpu.VMEM((groups,) + row_pair.shape, row_pair.dtype),
             pltpu.VMEM(row_query.shape, row_query.dtype),
-            pltpu.VMEM((2, pages - FORWARD_PAGES) + pool.shape[1:], pool.dtype),
+            pltpu.VMEM((3, pages - FORWARD_PAGES) + pool.shape[1:], pool.dtype),
             dma((5,)),
             dma((KV_HEAD_COUNT + 1,)),
             dma((4, 2)),
@@ -440,17 +491,28 @@
             dma((2, groups)),
             dma((2,)),
             dma((2,)),
+            dma((2,)),
+            dma((2,)),
+            dma((3, PIECES)),
+            dma((3, PIECES)),
             dma((PIECES,)),
             dma((PIECES,)),
-            dma((3, PIECES)),
-            dma((3, PIECES)),
         ],
-        compiler_params=pltpu.CompilerParams(collective_id=0, has_side_effects=True),
+        compiler_params=pltpu.CompilerParams(
+            collective_id=0, has_side_effects=True, vmem_limit_bytes=28 << 20
+        ),
         name="attention_and_moves",
-    )(arrival, table, lens, query, kv, row_query, row_pair, pool, move_table, move_len)
-
-
-LOAD_PARTS = 4
+    )(
+        arrival,
+        table,
+        lens,
+        *(
+            pltpu.with_memory_space_constraint(part, pltpu.HBM)
+            for part in (query, kv, row_query, row_pair, pool)
+        ),
+        move_table,
+        move_len,
+    )
 
 
 def place_kernel(
@@ -464,11 +526,7 @@
     decode_out,
     table,
     lens,
-    held,
     zero,
-    passed,
-    passed_row,
-    in_sems,
     out_sems,
     meta_sems,
     pass_sems,
@@ -478,46 +536,31 @@
         pltpu.make_async_copy(table_ref, table, meta_sems.at[0]),
         pltpu.make_async_copy(len_ref, lens, meta_sems.at[1]),
     ]
-    for copy in metas:
-        copy.start()
-    count = pages // LOAD_PARTS
-    parts = []
-    for index in range(LOAD_PARTS):
-        part = pl.ds(index * count, count)
-        parts.append(
-            pltpu.make_async_copy(raw_ref.at[part], held.at[part], in_sems.at[index])
-        )
-        parts[-1].start()
-    into = [
-        pltpu.make_async_copy(prefill_in, passed, pass_sems.at[0]),
-        pltpu.make_async_copy(decode_in, passed_row, pass_sems.at[1]),
+    passed = [
+        pltpu.make_async_copy(prefill_in, prefill_out, pass_sems.at[0]),
+        pltpu.make_async_copy(decode_in, decode_out, pass_sems.at[1]),
     ]
-    back = [
-        pltpu.make_async_copy(passed, prefill_out, pass_sems.at[2]),
-        pltpu.make_async_copy(passed_row, decode_out, pass_sems.at[3]),
-    ]
-    for copy in into:
+    for copy in metas + passed:
         copy.start()
     zero[...] = jnp.zeros_like(zero)
-    for copy in metas + parts:
+    for copy in metas:
         copy.wait()
     for i in range(pages):
         live = i * tokens < lens[0]
 
         @pl.when(live)
         def _():
-            pltpu.make_async_copy(held.at[table[0, i]], out_ref.at[i], out_sems.at[i]).start()
+            pltpu.make_async_copy(
+                raw_ref.at[table[0, i]], out_ref.at[i], out_sems.at[i]
+            ).start()
 
         @pl.when(jnp.logical_not(live))
         def _():
             pltpu.make_async_copy(zero, out_ref.at[i], out_sems.at[i]).start()
 
-    for first, second in zip(into, back):
-        first.wait()
-        second.start()
     for i in range(pages):
         pltpu.make_async_copy(zero, out_ref.at[i], out_sems.at[i]).wait()
-    for copy in back:
+    for copy in passed:
         copy.wait()
 
 
@@ -536,15 +579,12 @@
         scratch_shapes=[
             pltpu.SMEM(table.shape, table.dtype),
             pltpu.SMEM(lens.shape, lens.dtype),
-            pltpu.VMEM(raw.shape, raw.dtype),
             pltpu.VMEM(raw.shape[1:], raw.dtype),
-            pltpu.VMEM(prefill_rows.shape, prefill_rows.dtype),
-            pltpu.VMEM(decode_rows.shape, decode_rows.dtype),
-            dma((LOAD_PARTS,)),
             dma((pages,)),
             dma((2,)),
-            dma((4,)),
+            dma((2,)),
         ],
+        compiler_params=pltpu.CompilerParams(vmem_limit_bytes=8 << 20),
         name="place",
     )(table, lens, raw, prefill_rows, decode_rows)
 

time: 63.6 us -> 55.8 us (0.88)
  Pallas kernels: 62.2 us -> 52.7 us
  local copies, waits for them, and re-layouts: 0 us -> 1.3 us
    pallas_call x1, Pallas kernels: 57.8 us -> 50 us  [attention_and_moves(): pl.pallas_call(main_kernel, out_shape=(jax.ShapeDtypeStruct(query.shape,...]
    pallas_call x1, Pallas kernels: 4.4 us -> 2.77 us  [place(): pl.pallas_call(place_kernel, out_shape=tuple((jax.ShapeDtypeStruct(part.s...]
    unnamed x0 -> x4, local copies, waits for them, and re-layouts: none -> 1.3 us
where the time goes in v3:
time: 55.8 us; the launch traced here: 55.3 us
  Pallas kernels  52.7 us (94%)
  local copies, waits for them, and re-layouts  1.3 us (2%)
  between operations  1.3 us (2%)
    pallas_call x1, Pallas kernels, attention_and_moves(): pl.pallas_call(main_kernel, out_shape=(jax.ShapeDtypeStruct(query.shape,...  50 us
    pallas_call x1, Pallas kernels, place(): pl.pallas_call(place_kernel, out_shape=tuple((jax.ShapeDtypeStruct(part.s...  2.77 us
    unnamed x4, local copies, waits for them, and re-layouts  1.3 us

profile of v3, /device:TPU:4, one launch (start us, length us, event | category | flops | bytes accessed | tf_op | source)
XLA Modules:
  0.0 55.3 jit_solution(13891596449848700718)
XLA Ops:
  1.3 0.0 copy-start
  1.3 0.6 %copy-done = s32[1,32]{1,0:T(1,128)S(1)} copy-done((s32[1,32]{1,0:T(1,128)S(1)}, s32[1,32]{1,0:T(1,128)}, u32[]{:S(2)}) %copy-start) | copy-done | bytes 152
  1.9 0.0 copy-start.1
  1.9 0.7 %copy-done.1 = s32[32]{0:T(128)S(1)} copy-done((s32[32]{0:T(128)S(1)}, s32[32]{0:T(128)}, u32[]{:S(2)}) %copy-start.1) | copy-done | bytes 152
  2.6 50.0 %attention_and_moves.1 = (bf16[128,4096]{1,0:T(8,128)(2,1)S(1)}, bf16[1,512]{1,0:T(2,128)(2,1)S(1)}, bf16[32,128,256]{2,1,0:T(8,128)(2,1)S(1)}, s32[1,32]{1,0:T(1,128)S(1)}, s32[1]{0:T(128)}) custom-call(s32[32]{0:T(128)S(1)} %copy-done.1, s32[1,32]{1,0:T(1,128)S(1)} %copy-done, s32[1]{0:T(128)S(6)} %copy.11.len_ref.move_len_ref, ...), custom_call_target="tpu_custom_call" | custom-call | tf_op jit(solution)/shard_map/attention_and_moves/pallas_call | solution.py:464
  52.6 2.8 %place.1 = (bf16[32,128,256]{2,1,0:T(8,128)(2,1)}, bf16[128,4096]{1,0:T(8,128)(2,1)}, bf16[1,512]{1,0:T(2,128)(2,1)}) custom-call(s32[1,32]{1,0:T(1,128)S(1)} %get-tuple-element.11.table_ref, s32[1]{0:T(128)} %get-tuple-element.12.len_ref, bf16[32,128,256]{2,1,0:T(8,128)(2,1)S(1)} %get-tuple-element.13.raw_ref, ...), custom_call_target="tpu_custom_call" | custom-call | tf_op jit(solution)/shard_map/place/pallas_call | solution.py:571
Async XLA Ops:
  1.3 0.7 %copy-start = (s32[1,32]{1,0:T(1,128)S(1)}, s32[1,32]{1,0:T(1,128)}, u32[]{:S(2)}) copy-start(s32[1,32]{1,0:T(1,128)} %move_table_ref) | copy-start | bytes 388
  1.9 0.7 %copy-start.1 = (s32[32]{0:T(128)S(1)}, s32[32]{0:T(128)}, u32[]{:S(2)}) copy-start(s32[32]{0:T(128)} %arrival_ref.1) | copy-start | bytes 388

commit v4 on v3

--- a/solution.py
+++ b/solution.py
@@ -30,8 +30,8 @@
 
 
 def main_kernel(
-    arrival_ref,
-    table_ref,
+    arrival_in,
+    table_in,
     len_ref,
     query_ref,
     kv_ref,
@@ -53,6 +53,8 @@
     all_pair,
     decode_out,
     relays,
+    arrival_ref,
+    table_ref,
     load_sems,
     out_sems,
     kv_recv,
@@ -61,6 +63,8 @@
     part_send,
     row_recv,
     row_send,
+    round_recv,
+    round_send,
     meta_recv,
     meta_send,
     page_recv,
@@ -82,7 +86,7 @@
         return (group, 2 * c + core)
 
     def same_member(g):
-        return (g % groups, member)
+        return ((g + groups) % groups, member)
 
     partner = (group, 2 * x + 1 - core)
     next_group = same_member(group + 1)
@@ -101,13 +105,16 @@
         load(2, row_pair_ref, all_pair.at[group]),
         load(3, pool_ref, pool),
         load(4, query_ref, queries),
+        load(5, arrival_in, arrival_ref),
+        load(6, table_in, table_ref),
     ]
     for copy in loads:
         copy.start()
 
     barrier = pltpu.get_barrier_semaphore()
-    peers = [same_member(group + hop) for hop in range(1, groups)]
-    peers += [partner, chip_at((x + 1) % 4), chip_at((x + 3) % 4)]
+    peers = [partner, chip_at((x + 1) % 4), chip_at((x + 3) % 4)]
+    peers += [same_member(z * Y_CHIPS + (y + hop) % Y_CHIPS) for hop in range(1, Y_CHIPS)]
+    peers += [same_member(group + hop) for hop in (1, -1, Y_CHIPS, -Y_CHIPS)]
     for peer in peers:
         pl.semaphore_signal(barrier, inc=1, device_id=peer, device_id_type=MESH)
     pl.semaphore_wait(barrier, len(peers))
@@ -194,8 +201,30 @@
             target.at[group],
             row_send.at[index, hop],
             row_recv.at[index, hop],
-            same_member(group + hop),
-        )
+            same_member(z * Y_CHIPS + (y + hop) % Y_CHIPS),
+        )
+
+    def round_copy(index, hop):
+        first = ((z + hop) % Z_CHIPS) * Y_CHIPS
+        block = (all_query, all_pair)[index].at[pl.ds(first, Y_CHIPS)]
+        return remote(
+            block,
+            block,
+            round_send.at[index, hop],
+            round_recv.at[index, hop],
+            same_member(group - Y_CHIPS),
+        )
+
+    def pass_rows(hop):
+        for index in range(2):
+            if hop == 0:
+                loads[1 + index].wait()
+                for other in range(1, Y_CHIPS):
+                    row_copy(index, other).wait()
+            else:
+                round_copy(index, hop - 1).wait_recv()
+            if hop < Z_CHIPS - 1:
+                round_copy(index, hop).start()
 
     def kv_copy(c, half, target, lane):
         return remote(
@@ -226,7 +255,7 @@
     for half in range(2):
         part_copy(x, half).start()
 
-    for hop in range(1, groups):
+    for hop in range(1, Y_CHIPS):
         for index in range(2):
             row_copy(index, hop).start()
     metas = [
@@ -287,6 +316,7 @@
 
     first_relay(0)
     first_relay(1)
+    pass_rows(0)
 
     @pl.when(x == 1)
     def _():
@@ -310,10 +340,12 @@
         arrived(1, 1)
         kv_copy(1, 1, chip_at(3), 4).start()
 
+    first_relay(2)
     raised_relay(0)
-    first_relay(2)
+    pass_rows(1)
+    first_relay(3)
     raised_relay(1)
-    first_relay(3)
+    pass_rows(2)
 
     @pl.when(x == 1)
     def _():
@@ -330,17 +362,10 @@
         part_copy(0, 1).start()
         take(2, 1)
 
-    for copy in loads[1:4]:
-        copy.wait()
-    for hop in range(1, groups):
-        for index in range(2):
-            row_copy(index, hop).wait()
-    attend_decode()
-    decode_store = pltpu.make_async_copy(decode_out, decode_ref, out_sems.at[KV_HEAD_COUNT])
-    decode_store.start()
-
+    pass_rows(3)
     raised_relay(2)
     last_relay(0)
+    pass_rows(4)
     raised_relay(3)
 
     @pl.when(x == 2)
@@ -354,6 +379,7 @@
         take(1, 1)
 
     last_relay(1)
+    pass_rows(5)
     for c in range(4):
 
         @pl.when(c <= x)
@@ -410,12 +436,20 @@
 
     def attend_then_relay(n, carry):
         attend_head(n, carry)
+        pl.when(n == 0)(functools.partial(pass_rows, 6))
         pl.when(n == 1)(functools.partial(last_relay, 2))
         pl.when(n == 3)(functools.partial(last_relay, 3))
         return carry
 
     lax.fori_loop(0, KV_HEAD_COUNT, attend_then_relay, 0)
 
+    pass_rows(7)
+    for index in (3, 5, 6):
+        loads[index].wait()
+    attend_decode()
+    decode_store = pltpu.make_async_copy(decode_out, decode_ref, out_sems.at[KV_HEAD_COUNT])
+    decode_store.start()
+
     @pl.when(x == 0)
     def _():
         for lane in range(5):
@@ -440,6 +474,9 @@
     lax.fori_loop(0, KV_HEAD_COUNT, out_wait, 0)
     for copy in metas:
         copy.wait()
+    for index in range(2):
+        for hop in range(Z_CHIPS - 1):
+            round_copy(index, hop).wait_send()
     for index in range(PIECES):
         for step in range(3):
             relay_copy(step, index).wait_send()
@@ -451,13 +488,16 @@
         relay_copy(2, index).wait_recv()
     for index in range(2):
         straight_copy(index).wait()
+
+
+def in_hbm(array):
+    return pltpu.with_memory_space_constraint(array, pltpu.HBM)
 
 
 def attention_and_moves(
     arrival, table, lens, query, kv, row_query, row_pair, pool, move_table, move_len
 ):
     any_space = pl.BlockSpec(memory_space=pl.ANY)
-    smem = pl.BlockSpec(memory_space=pltpu.SMEM)
     dma = pltpu.SemaphoreType.DMA
     groups = Y_CHIPS * Z_CHIPS
     pages = pool.shape[0]
@@ -470,7 +510,7 @@
             jax.ShapeDtypeStruct(move_table.shape, move_table.dtype),
             jax.ShapeDtypeStruct(move_len.shape, move_len.dtype),
         ),
-        in_specs=[smem] * 3 + [any_space] * 7,
+        in_specs=[any_space] * 2 + [pl.BlockSpec(memory_space=pltpu.SMEM)] + [any_space] * 7,
         out_specs=(any_space,) * 5,
         scratch_shapes=[
             pltpu.VMEM(query.shape, query.dtype),
@@ -481,14 +521,18 @@
             pltpu.VMEM((groups,) + row_pair.shape, row_pair.dtype),
             pltpu.VMEM(row_query.shape, row_query.dtype),
             pltpu.VMEM((3, pages - FORWARD_PAGES) + pool.shape[1:], pool.dtype),
-            dma((5,)),
+            pltpu.SMEM(arrival.shape, arrival.dtype),
+            pltpu.SMEM(table.shape, table.dtype),
+            dma((7,)),
             dma((KV_HEAD_COUNT + 1,)),
             dma((4, 2)),
             dma((5,)),
             dma((4, 2)),
             dma((4, 2)),
-            dma((2, groups)),
-            dma((2, groups)),
+            dma((2, Y_CHIPS)),
+            dma((2, Y_CHIPS)),
+            dma((2, Z_CHIPS)),
+            dma((2, Z_CHIPS)),
             dma((2,)),
             dma((2,)),
             dma((2,)),
@@ -503,14 +547,15 @@
         ),
         name="attention_and_moves",
     )(
-        arrival,
-        table,
+        in_hbm(arrival),
+        in_hbm(table),
         lens,
-        *(
-            pltpu.with_memory_space_constraint(part, pltpu.HBM)
-            for part in (query, kv, row_query, row_pair, pool)
-        ),
-        move_table,
+        in_hbm(query),
+        in_hbm(kv),
+        in_hbm(row_query),
+        in_hbm(row_pair),
+        in_hbm(pool),
+        in_hbm(move_table),
         move_len,
     )
 

time: 55.8 us -> 50.8 us (0.910)
  the two profiles are of different devices: /device:TPU:4 before, /device:TPU:1 now
where the time goes in v4:
time: 50.8 us; the launch traced here: 50.7 us
  Pallas kernels  49.4 us (97%)
  between operations  1.29 us (3%)
    pallas_call x1, Pallas kernels, attention_and_moves(): pl.pallas_call(main_kernel, out_shape=(jax.ShapeDtypeStruct(query.shape,...  46.6 us
    pallas_call x1, Pallas kernels, place(): pl.pallas_call(place_kernel, out_shape=tuple((jax.ShapeDtypeStruct(part.s...  2.79 us

profile of v4, /device:TPU:1, one launch (start us, length us, event | category | flops | bytes accessed | tf_op | source)
XLA Modules:
  0.0 50.7 jit_solution(15654545202283916966)
XLA Ops:
  1.3 46.6 %attention_and_moves.1 = (bf16[128,4096]{1,0:T(8,128)(2,1)S(1)}, bf16[1,512]{1,0:T(2,128)(2,1)S(1)}, bf16[32,128,256]{2,1,0:T(8,128)(2,1)S(1)}, s32[1,32]{1,0:T(1,128)S(1)}, s32[1]{0:T(128)}) custom-call(s32[32]{0:T(128)} %arrival_in.1, s32[1,32]{1,0:T(1,128)} %move_table_ref, s32[1]{0:T(128)S(6)} %copy.11.len_ref.move_len_ref, bf16[128,4096]{1,0:T(8,128)(2,1)} %query_ref.1, ...), custom_call_target="tpu_custom_call" | custom-call | tf_op jit(solution)/shard_map/attention_and_moves/pallas_call | solution.py:504
  47.9 2.8 %place.1 = (bf16[32,128,256]{2,1,0:T(8,128)(2,1)}, bf16[128,4096]{1,0:T(8,128)(2,1)}, bf16[1,512]{1,0:T(2,128)(2,1)}) custom-call(s32[1,32]{1,0:T(1,128)S(1)} %get-tuple-element.11.table_ref, s32[1]{0:T(128)} %get-tuple-element.12.len_ref, bf16[32,128,256]{2,1,0:T(8,128)(2,1)S(1)} %get-tuple-element.13.raw_ref, ...), custom_call_target="tpu_custom_call" | custom-call | tf_op jit(solution)/shard_map/place/pallas_call | solution.py:616
